TPU v7x, 32 devices: a whole 2x2x4 slice. The times are simulated.
32 devices in a mesh: row: 4 (over x, core), col: 8 (over z, y).
Axes of the slice: x: 2, y: 2, z: 4, core: 2. Of those that a mesh axis runs over, the one named last changes fastest.
Arguments:
- matrix: float32 [2048, 2048], P('row', 'col'), as said below
- panel: float32 [2048, 256], P(('row', 'col')), may hold values from -0.125 to 0.125
- factor: float32 [256, 256], replicated, as said below
Outputs:
- updated: float32 [2048, 2048], P('row', 'col')
- correction: float32 [2048, 256], P(('row', 'col'))
Inputs may be any that keep to these rules, and one draw needn't show every extreme that they name: `matrix`: symmetric. `factor`: upper triangular with a positive diagonal.
All inputs are finite; a program needn't handle non-finite values.
Results may differ from a plain program's by a relative error of at most 0.000071.
Values sent between devices are 32-bit elements; how exact they have to be, the bound alone decides.
A program may use at most 64 MiB of HBM per device.

v0:
```python
import functools

import jax
import jax.numpy as jnp
from jax import lax
from jax.experimental import pallas as pl
from jax.experimental.pallas import tpu as pltpu
from jax.sharding import PartitionSpec as P

F32 = jnp.float32
BF16 = jnp.bfloat16
NN = (((1,), (0,)), ((), ()))
NT = (((1,), (1,)), ((), ()))


def split(x):
    high = x.astype(BF16)
    return high, (x - high.astype(F32)).astype(BF16)


def mult(a, b, dims=NN):
    dot = functools.partial(lax.dot_general, dimension_numbers=dims, preferred_element_type=F32)
    return dot(a[0], b[1]) + dot(a[1], b[0]) + dot(a[0], b[0])


def tile_loop(count, body):
    if count <= 2:
        for i in range(count):
            body(i)
    else:
        pl.loop(0, count)(body)


def kernel(nrows, ncols, tile, a_ref, panel_ref, t_ref, out_ref, corr_ref,
           vr, vc, sr, sc, q, qin, kpart, kin, kpair, kfull, at_hi, at_lo, vt_hi, vt_lo,
           v_send, v_recv, vf_send, vf_recv, q_send, q_recv, sc_send, sc_recv,
           s_send, s_recv, sf_send, sf_recv, vc_send, vc_recv, k_send, k_recv, kg_send, kg_recv):
    r, c = lax.axis_index("row"), lax.axis_index("col")
    lines = ncols // 2
    group = ncols // (2 * nrows)
    z, y = c // 2, c % 2
    blk, width = panel_ref.shape
    total = a_ref.shape[0]
    tiles = total // tile
    half = width // 2
    mate = r + 1 - 2 * (r % 2)

    def rows(index, size):
        return pl.ds(pl.multiple_of(index * size, size), size)

    def copy(src, dst, send, recv, row, col):
        return pltpu.make_async_remote_copy(
            src_ref=src, dst_ref=dst, send_sem=send, recv_sem=recv,
            device_id=(row, col), device_id_type=pl.DeviceIdType.MESH)

    barrier = pltpu.get_barrier_semaphore()

    def greet(row, col):
        pl.semaphore_signal(barrier, inc=1, device_id=(row, col), device_id_type=pl.DeviceIdType.MESH)

    target = z // group
    for d in range(1, lines):
        greet(r, lax.rem(z + d, lines) * 2 + y)
    greet(r, z * 2 + 1 - y)
    opposite = lax.rem(z + lines // 2, lines)
    greet(r, opposite * 2 + 1 - y)
    for d in range(1, nrows):
        greet(lax.rem(r + d, nrows), c)
    for g in range(group):
        line = r * group + g

        @pl.when(z != line)
        def _():
            for d in range(1, nrows):
                greet(lax.rem(r + d, nrows), line * 2 + y)

    vr[rows(c, blk), :] = panel_ref[...]
    pl.semaphore_wait(barrier, lines + nrows + jnp.where(target == r, 0, lines - 1))
    sends = []
    holder = c * nrows // ncols
    first_block = lax.rem(c * nrows, ncols)

    def each_line(body, sign, skip=0):
        for d in range(1, lines):
            if d == skip:
                continue
            body(lax.rem(z + sign * d + lines, lines))

    def finish():
        for desc in sends:
            desc.wait_send()
        for d in range(lines):
            line = lax.rem(z + d, lines)
            copy(panel_ref, panel_ref, v_send.at[line], v_recv.at[line], r, c).wait_send()
            if d:
                copy(panel_ref, panel_ref, vf_send.at[line], vf_recv.at[line], r, c).wait_send()
                copy(panel_ref, panel_ref, s_send.at[line], s_recv.at[0], r, c).wait_send()

        for i in range(nrows * group):
            copy(panel_ref, panel_ref, sf_send.at[i], sf_recv.at[i], r, c).wait_send()

        @pl.when(r % 2 == holder % 2)
        def _():
            copy(vc, vc, vc_send.at[0], vc_recv.at[0], r, c).wait_send()

        @pl.when(r == holder)
        def _():
            for d in range(1, nrows // 2):
                copy(vc, vc, vc_send.at[d], vc_recv.at[0], r, c).wait_send()

    def go(desc):
        desc.start()
        sends.append(desc)

    across = z * 2 + 1 - y
    own = vr.at[rows(c, blk)]
    copy(panel_ref, own, v_send.at[z], v_recv.at[z], r, across).start()

    def send_panel(line):
        copy(panel_ref, own, v_send.at[line], v_recv.at[z], r, line * 2 + y).start()
    each_line(send_panel, 1)
    copy(panel_ref, own, vf_send.at[opposite], vf_recv.at[z], r, opposite * 2 + 1 - y).start()

    def flip(i):
        lo_i = pl.ds(pl.multiple_of(i * tile, tile), tile)
        high, low = split(a_ref[lo_i, :].T)
        at_hi[i] = high
        at_lo[i] = low
    tile_loop(tiles, flip)
    t_two = split(t_ref[...])

    def forward(line):
        slot = vr.at[rows(line * 2 + y, blk)]
        copy(slot, slot, v_send.at[line], v_recv.at[line], r, c).wait_recv()
        copy(slot, slot, vf_send.at[line], vf_recv.at[line], r, across).start()

    def arrive(line):
        slot = vr.at[rows(line * 2 + 1 - y, blk)]
        copy(slot, slot, vf_send.at[line], vf_recv.at[line], r, c).wait_recv()

    each_line(forward, -1, lines // 2)
    slot = vr.at[rows(opposite * 2 + y, blk)]
    copy(slot, slot, v_send.at[opposite], v_recv.at[opposite], r, c).wait_recv()
    slot = vr.at[rows(across, blk)]
    copy(slot, slot, v_send.at[z], v_recv.at[z], r, c).wait_recv()
    each_line(arrive, -1)

    q[...] = jnp.zeros_like(q)

    def gather_product(i):
        q[...] += mult((at_hi[i], at_lo[i]), split(vr[pl.ds(pl.multiple_of(i * tile, tile), tile), :]))
    tile_loop(tiles, gather_product)

    for d in range(1, nrows):
        other = lax.rem(r + d, nrows)
        go(copy(q.at[rows(other, blk)], qin.at[d], q_send.at[d], q_recv.at[d], other, c))

    def turn(i):
        high, low = split(mult(split(vr[pl.ds(pl.multiple_of(i * tile, tile), tile), :]), t_two).T)
        vt_hi[i] = high
        vt_lo[i] = low
    tile_loop(tiles, turn)

    for d in range(1, nrows):
        copy(qin.at[d], qin.at[d], q_send.at[d], q_recv.at[d], r, c).wait_recv()
    product = q[rows(r, blk), :]
    for d in range(1, nrows):
        product = product + qin[d]
    mine = sc.at[rows(r, blk)]
    sc[rows(r, blk), :] = mult(split(product), t_two)

    local = lax.rem(c * nrows + r, ncols)
    here = r * group + lax.rem(z, group)

    def send_scaled(line):
        copy(mine, sr.at[rows(local, blk)], s_send.at[line], s_recv.at[here], target, line * 2 + y).start()
    each_line(send_scaled, 1)
    for d in range(1, nrows):
        go(copy(mine, mine, sc_send.at[d], sc_recv.at[d], lax.rem(r + d, nrows), c))

    for d in range(1, nrows):
        slot = sc.at[rows(lax.rem(r - d + nrows, nrows), blk)]
        copy(slot, slot, sc_send.at[d], sc_recv.at[d], r, c).wait_recv()

    for g in range(group):
        line = r * group + g
        for d in range(nrows):
            j = lax.rem(r + d, nrows)
            place = lax.rem((line * 2 + y) * nrows + j, ncols)
            slot = sr.at[rows(place, blk)]

            @pl.when(z == line)
            def _():
                held = sc.at[rows(j, blk)]
                copy(held, slot, sf_send.at[j * group + g], sf_recv.at[j * group + g], r, across).start()
                slot[...] = held[...]

            @pl.when(z != line)
            def _():
                copy(slot, slot, s_send.at[0], s_recv.at[j * group + g], r, c).wait_recv()
                copy(slot, slot, sf_send.at[j * group + g], sf_recv.at[j * group + g], r, across).start()
    @pl.when(r == holder)
    def _():
        v_slice = vr.at[rows(first_block // nrows, nrows * blk)]
        for d in range(1, nrows // 2):
            copy(v_slice, vc, vc_send.at[d], vc_recv.at[0], lax.rem(r + 2 * d, nrows), c).start()
        copy(v_slice, vc, vc_send.at[0], vc_recv.at[0], mate, c).start()
        vc[...] = v_slice[...]

    for g in range(group):
        line = r * group + g
        for j in range(nrows):
            place = lax.rem((line * 2 + 1 - y) * nrows + j, ncols)
            slot = sr.at[rows(place, blk)]
            copy(slot, slot, sf_send.at[j * group + g], sf_recv.at[j * group + g], r, c).wait_recv()

    kpart[...] = jnp.zeros_like(kpart)

    def inner(i):
        kpart[...] += mult((vt_hi[i], vt_lo[i]), split(sr[pl.ds(pl.multiple_of(i * tile, tile), tile), :]))
    tile_loop(tiles, inner)

    go(copy(kpart.at[rows(mate % 2, half)], kin.at[0], k_send.at[0], k_recv.at[0], mate, c))

    @pl.when(r != holder)
    def _():
        copy(vc, vc, vc_send.at[0], vc_recv.at[0], r, c).wait_recv()

    @pl.when((r != holder) & (r % 2 == holder % 2))
    def _():
        copy(vc, vc, vc_send.at[0], vc_recv.at[0], mate, c).start()

    copy(kin.at[0], kin.at[0], k_send.at[0], k_recv.at[0], r, c).wait_recv()
    kpair[...] = kpart[rows(r % 2, half), :] + kin[0]
    for d in range(1, nrows // 2):
        go(copy(kpair, kin.at[d], k_send.at[d], k_recv.at[d], lax.rem(r + 2 * d, nrows), c))

    vc_two = split(vc[...])

    def first(i):
        span = pl.ds(pl.multiple_of(i * tile, tile), tile)
        out_ref[span, :] = a_ref[span, :] - mult(split(sr[span, :]), vc_two, NT)
    tile_loop(tiles, first)

    for d in range(1, nrows // 2):
        copy(kpair, kin.at[d], k_send.at[d], k_recv.at[d], r, c).wait_recv()
    summed = kpair[...]
    for d in range(1, nrows // 2):
        summed = summed + kin[d]
    mine_half = kfull.at[rows(r % 2, half)]
    mine_half[...] = summed
    go(copy(mine_half, mine_half, kg_send.at[0], kg_recv.at[0], mate, c))
    other_half = kfull.at[rows(mate % 2, half)]
    copy(other_half, other_half, kg_send.at[0], kg_recv.at[0], r, c).wait_recv()

    k_two = split(kfull[...])
    y_two = split(sc[...] - mult(vc_two, k_two))

    def second(i):
        span = pl.ds(pl.multiple_of(i * tile, tile), tile)
        out_ref[span, :] = out_ref[span, :] - mult(split(vr[span, :]), y_two, NT)
    tile_loop(tiles, second)
    corr_ref[...] = sr[rows(c, blk), :] - 0.5 * mult(split(panel_ref[...]), k_two)

    finish()


def hand_out(held_ref, held_corr_ref, out_ref, corr_ref):
    out_ref[...] = held_ref[...]
    corr_ref[...] = held_corr_ref[...]


def per_device(nrows, ncols, matrix, panel, factor):
    total, wide = matrix.shape
    blk, width = panel.shape
    tile = min(256, total)
    tiles = total // tile
    group = ncols // (2 * nrows)
    lines = ncols // 2
    dma = pltpu.SemaphoreType.DMA
    vmem = pl.BlockSpec(memory_space=pltpu.VMEM)
    limit = 4 * (5 * total * wide + 4 * total * width + 4 * wide * width + 16 * width * width) + (4 << 20)
    held = pl.pallas_call(
        functools.partial(kernel, nrows, ncols, tile),
        out_shape=(jax.ShapeDtypeStruct(matrix.shape, F32), jax.ShapeDtypeStruct(panel.shape, F32)),
        in_specs=[vmem] * 3,
        out_specs=(vmem, vmem),
        scratch_shapes=[
            pltpu.VMEM((total, width), F32),
            pltpu.VMEM((wide, width), F32),
            pltpu.VMEM((total, width), F32),
            pltpu.VMEM((wide, width), F32),
            pltpu.VMEM((wide, width), F32),
            pltpu.VMEM((nrows, blk, width), F32),
            pltpu.VMEM((width, width), F32),
            pltpu.VMEM((nrows // 2, width // 2, width), F32),
            pltpu.VMEM((width // 2, width), F32),
            pltpu.VMEM((width, width), F32),
            pltpu.VMEM((tiles, wide, tile), BF16),
            pltpu.VMEM((tiles, wide, tile), BF16),
            pltpu.VMEM((tiles, width, tile), BF16),
            pltpu.VMEM((tiles, width, tile), BF16),
            dma((lines,)), dma((lines,)), dma((lines,)), dma((lines,)),
            dma((nrows,)), dma((nrows,)), dma((nrows,)), dma((nrows,)),
            dma((lines,)), dma((nrows * group,)), dma((nrows * group,)), dma((nrows * group,)),
            dma((nrows,)), dma((1,)), dma((nrows,)), dma((nrows,)), dma((nrows,)), dma((nrows,)),
        ],
        compiler_params=pltpu.CompilerParams(
            collective_id=0, has_side_effects=True, vmem_limit_bytes=limit),
    )(matrix, panel, factor)
    return pl.pallas_call(
        hand_out,
        out_shape=(jax.ShapeDtypeStruct(matrix.shape, F32), jax.ShapeDtypeStruct(panel.shape, F32)),
        in_specs=[vmem] * 2,
        out_specs=(vmem, vmem),
        compiler_params=pltpu.CompilerParams(vmem_limit_bytes=6 * total * wide * 4 + (1 << 20)),
    )(*held)


def solution(mesh):
    in_specs = (P("row", "col"), P(("row", "col"), None), P())
    out_specs = (P("row", "col"), P(("row", "col"), None))
    return jax.shard_map(
        functools.partial(per_device, mesh.shape["row"], mesh.shape["col"]),
        mesh=mesh, in_specs=in_specs, out_specs=out_specs, check_vma=False)
```

profile of v0, /device:TPU:5, one launch (start us, length us, event | category | flops | bytes accessed | tf_op | source)
XLA Modules:
  0.0 47.3 jit_solution(15765128918739029024)
XLA Ops:
  0.6 0.0 copy-start
  0.6 1.0 %copy-done = f32[512,256]{1,0:T(8,128)S(1)} copy-done((f32[512,256]{1,0:T(8,128)S(1)}, f32[512,256]{1,0:T(8,128)}, u32[]{:S(2)}) %copy-start) | copy-done | bytes 524312
  1.7 0.0 copy-start.1
  1.7 0.9 %copy-done.1 = f32[256,256]{1,0:T(8,128)S(1)} copy-done((f32[256,256]{1,0:T(8,128)S(1)}, f32[256,256]{1,0:T(8,128)}, u32[]{:S(2)}) %copy-start.1) | copy-done | bytes 262168
  2.6 0.0 copy-start.2
  2.6 0.8 %copy-done.2 = f32[64,256]{1,0:T(8,128)S(1)} copy-done((f32[64,256]{1,0:T(8,128)S(1)}, f32[64,256]{1,0:T(8,128)}, u32[]{:S(2)}) %copy-start.2) | copy-done | bytes 65560
  3.5 43.0 %shard_map.50 = (f32[512,256]{1,0:T(8,128)S(1)}, f32[64,256]{1,0:T(8,128)S(1)}) custom-call(f32[512,256]{1,0:T(8,128)S(1)} %copy-done, f32[64,256]{1,0:T(8,128)S(1)} %copy-done.2, f32[256,256]{1,0:T(8,128)S(1)} %copy-done.1), custom_call_target="tpu_custom_call" | custom-call | tf_op jit(solution)/shard_map/pallas_call | solution.py:283
  46.5 0.8 %shard_map.51 = (f32[512,256]{1,0:T(8,128)}, f32[64,256]{1,0:T(8,128)}) custom-call(f32[512,256]{1,0:T(8,128)S(1)} %get-tuple-element.4.held_ref, f32[64,256]{1,0:T(8,128)S(1)} %get-tuple-element.5.held_corr_ref), custom_call_target="tpu_custom_call" | custom-call | tf_op jit(solution)/shard_map/pallas_call | solution.py:311
Async XLA Ops:
  0.6 1.0 %copy-start = (f32[512,256]{1,0:T(8,128)S(1)}, f32[512,256]{1,0:T(8,128)}, u32[]{:S(2)}) copy-start(f32[512,256]{1,0:T(8,128)} %a_ref.1) | copy-start | bytes 1572868
  1.7 0.9 %copy-start.1 = (f32[256,256]{1,0:T(8,128)S(1)}, f32[256,256]{1,0:T(8,128)}, u32[]{:S(2)}) copy-start(f32[256,256]{1,0:T(8,128)} %t_ref.1) | copy-start | bytes 786436
  2.6 0.8 %copy-start.2 = (f32[64,256]{1,0:T(8,128)S(1)}, f32[64,256]{1,0:T(8,128)}, u32[]{:S(2)}) copy-start(f32[64,256]{1,0:T(8,128)} %panel_ref.1) | copy-start | bytes 196612
where the time goes:
time: 47.6 us; the launch traced here: 47.3 us
  Pallas kernels  43.8 us (92%)
  local copies, waits for them, and re-layouts  2.82 us (6%)
  between operations  0.65 us (1%)
    pallas_call x1, Pallas kernels, per_device(): pl.pallas_call(functools.partial(kernel, nrows, ncols, tile), out_shape=(...  43 us
    unnamed x6, local copies, waits for them, and re-layouts  2.82 us

commit v1 on v0

v1 whole, which is shorter than its diff:
```python
import functools

import jax
import jax.numpy as jnp
from jax import lax
from jax.experimental import pallas as pl
from jax.experimental.pallas import tpu as pltpu
from jax.sharding import PartitionSpec as P

F32 = jnp.float32
BF16 = jnp.bfloat16
NN = (((1,), (0,)), ((), ()))
NT = (((1,), (1,)), ((), ()))


def split(x):
    high = x.astype(BF16)
    return high, (x - high.astype(F32)).astype(BF16)


def mult(a, b, dims=NN):
    dot = functools.partial(lax.dot_general, dimension_numbers=dims, preferred_element_type=F32)
    return dot(a[0], b[1]) + dot(a[1], b[0]) + dot(a[0], b[0])


def wide_of(ref, span):
    return jnp.concatenate([ref[0, span, :], ref[1, span, :]], axis=1)


def tile_loop(count, body):
    if count <= 2:
        for i in range(count):
            body(i)
    else:
        pl.loop(0, count)(body)


def kernel(nrows, ncols, tile, a_hbm, panel_hbm, t_hbm, out_ref, corr_ref,
           a_ref, t_ref, vr, vc, sr, sc, q, qin, kpart, kin, kpair, kfull, klast, klin,
           at_hi, at_lo, vt_hi, vt_lo,
           local_sem, v_send, v_recv, vf_send, vf_recv, q_send, q_recv,
           s_send, s_recv, sd_send, sf_send, sf_recv, sc_send, sc_recv,
           vc_send, vc_recv, k_send, k_recv, kg_send, kg_recv, kl_send, kl_recv):
    r, c = lax.axis_index("row"), lax.axis_index("col")
    lines = ncols // 2
    group = ncols // (2 * nrows)
    z, y = c // 2, c % 2
    total = a_ref.shape[0]
    nh, wide, hw = sc.shape
    blk, width = panel_hbm.shape
    tiles = total // tile
    half = width // 2
    mate = r + 1 - 2 * (r % 2)
    far = lines // 2

    def rows(index, size):
        return pl.ds(pl.multiple_of(index * size, size), size)

    def peer(d):
        line = z
        for b in range(lines.bit_length()):
            if d >> b & 1:
                line = line + (1 << b) - (2 << b) * (z // (1 << b) % 2)
        return line

    def copy(src, dst, send, recv, row, col):
        return pltpu.make_async_remote_copy(
            src_ref=src, dst_ref=dst, send_sem=send, recv_sem=recv,
            device_id=(row, col), device_id_type=pl.DeviceIdType.MESH)

    sends = []

    def go(desc, when=None):
        if when is None:
            desc.start()
        else:
            pl.when(when)(desc.start)
        sends.append((desc, when))

    opposite = peer(far)
    across = z * 2 + 1 - y
    target = z // group
    barrier = pltpu.get_barrier_semaphore()

    def greet(row, col):
        pl.semaphore_signal(barrier, inc=1, device_id=(row, col), device_id_type=pl.DeviceIdType.MESH)

    for d in range(1, lines):
        greet(r, peer(d) * 2 + y)
    greet(r, across)
    greet(r, opposite * 2 + 1 - y)
    for d in range(1, nrows):
        greet(lax.rem(r + d, nrows), c)
    for g in range(group):
        line = r * group + g

        @pl.when(z != line)
        def _():
            for d in range(1, nrows):
                greet(lax.rem(r + d, nrows), line * 2 + y)

        @pl.when(opposite == line)
        def _():
            for d in range(1, nrows):
                greet(lax.rem(r + d, nrows), line * 2 + 1 - y)

    loads = [pltpu.make_async_copy(panel_hbm.at[:, pl.ds(h * hw, hw)], vr.at[h, rows(c, blk), :], local_sem.at[h])
             for h in range(nh)]
    loads.append(pltpu.make_async_copy(a_hbm, a_ref, local_sem.at[nh]))
    loads.append(pltpu.make_async_copy(t_hbm, t_ref, local_sem.at[nh + 1]))
    for load in loads:
        load.start()
    for h in range(nh):
        loads[h].wait()
    pl.semaphore_wait(barrier, lines + nrows + jnp.where(target == r, 0, lines))

    order = [d for d in reversed(range(1, lines)) if d != far] + [far]
    for h in range(nh):
        own = vr.at[h, rows(c, blk), :]
        go(copy(own, own, v_send.at[h, z], v_recv.at[h, z], r, across))
        for d in order:
            go(copy(own, own, v_send.at[h, peer(d)], v_recv.at[h, z], r, peer(d) * 2 + y))
        go(copy(own, own, vf_send.at[h, opposite], vf_recv.at[h, z], r, opposite * 2 + 1 - y))

    loads[nh].wait()

    def flip(i):
        high, low = split(a_ref[pl.ds(pl.multiple_of(i * tile, tile), tile), :].T)
        at_hi[i] = high
        at_lo[i] = low
    tile_loop(tiles, flip)
    loads[nh + 1].wait()
    t_two = split(t_ref[...])
    tt_two = split(t_ref[...].T)

    def arrived(h, line, side, recv):
        slot = vr.at[h, rows(line * 2 + side, blk), :]
        copy(slot, slot, v_send.at[h, line], recv.at[h, line], r, c).wait_recv()
        return slot

    for h in range(nh):
        for d in range(1, lines):
            if d != far:
                line = peer(d)
                slot = arrived(h, line, y, v_recv)
                go(copy(slot, slot, vf_send.at[h, line], vf_recv.at[h, line], r, across))

    def reduce_product(h):
        for e in range(tiles):
            for d in (2 * e, 2 * e + 1):
                line = peer(d)
                if d == far:
                    arrived(h, line, y, v_recv)
                arrived(h, line, 1 - y, vf_recv if d else v_recv)
            i = peer(2 * e) // 2
            part = mult((at_hi[i], at_lo[i]), split(vr[h, rows(i, tile), :]))
            q[h] = part if e == 0 else q[h] + part
        for d in range(1, nrows):
            other = lax.rem(r + d, nrows)
            go(copy(q.at[h, rows(other, blk), :], qin.at[h, d], q_send.at[h, d], q_recv.at[h, d], other, c))

    for h in range(nh):
        reduce_product(h)

    def turn(i):
        span = pl.ds(pl.multiple_of(i * tile, tile), tile)
        high, low = split(mult(tt_two, split(wide_of(vr, span)), NT))
        vt_hi[i] = high
        vt_lo[i] = low
    tile_loop(tiles, turn)

    place = lax.rem(c * nrows + r, ncols)
    here = r * group + lax.rem(z, group)
    products = []
    for h in range(nh):
        for d in range(1, nrows):
            copy(qin.at[h, d], qin.at[h, d], q_send.at[h, d], q_recv.at[h, d], r, c).wait_recv()
        product = q[h, rows(r, blk), :]
        for d in range(1, nrows):
            product = product + qin[h, d]
        products.append(split(product))
        scaled = None
        for g in range(h + 1):
            block = tuple(t[g * hw:(g + 1) * hw, h * hw:(h + 1) * hw] for t in t_two)
            term = mult(products[g], block)
            scaled = term if scaled is None else scaled + term
        mine = sc.at[h, rows(r, blk), :]
        mine[...] = scaled
        slot = sr.at[h, rows(place, blk), :]
        for d in order:
            go(copy(mine, slot, s_send.at[h, peer(d)], s_recv.at[h, here], target, peer(d) * 2 + y))
        go(copy(mine, slot, sd_send.at[h], sf_recv.at[h, here], target, opposite * 2 + 1 - y))
        for d in range(1, nrows):
            go(copy(mine, mine, sc_send.at[h, d], sc_recv.at[h, d], lax.rem(r + d, nrows), c))

    holder = c * nrows // ncols
    first_block = lax.rem(c * nrows, ncols)
    v_slice = vr.at[:, rows(first_block // nrows, wide), :]
    same = r % 2 == holder % 2
    for d in range(1, nrows // 2):
        go(copy(v_slice, vc, vc_send.at[d], vc_recv.at[0], lax.rem(r + 2 * d, nrows), c), r == holder)
    to_mate = copy(v_slice, vc, vc_send.at[0], vc_recv.at[0], mate, c)

    @pl.when(r == holder)
    def _():
        to_mate.start()
        vc[...] = v_slice[...]

    def forward_scaled(h):
        for d in range(1, nrows):
            slot = sc.at[h, rows(lax.rem(r - d + nrows, nrows), blk), :]
            copy(slot, slot, sc_send.at[h, d], sc_recv.at[h, d], r, c).wait_recv()
        for g in range(group):
            line = r * group + g
            for d in range(nrows):
                j = lax.rem(r + d, nrows)
                at = j * group + g
                slot = sr.at[h, rows(lax.rem((line * 2 + y) * nrows + j, ncols), blk), :]
                held = sc.at[h, rows(j, blk), :]
                straight = copy(held, slot, sf_send.at[h, at], sf_recv.at[h, at], r, across)
                passed = copy(slot, slot, sf_send.at[h, at], sf_recv.at[h, at], r, across)
                came = copy(slot, slot, s_send.at[h, 0], s_recv.at[h, at], r, c)

                @pl.when(z == line)
                def _():
                    straight.start()
                    slot[...] = held[...]

                @pl.when(z != line)
                def _():
                    came.wait_recv()

                    @pl.when(opposite != line)
                    def _():
                        passed.start()
                sends.append((passed, opposite != line))

    def gather_scaled(h):
        for g in range(group):
            line = r * group + g
            for j in range(nrows):
                at = j * group + g
                slot = sr.at[h, rows(lax.rem((line * 2 + 1 - y) * nrows + j, ncols), blk), :]
                copy(slot, slot, sf_send.at[h, at], sf_recv.at[h, at], r, c).wait_recv()

    for h in range(nh):
        forward_scaled(h)

    gather_scaled(0)
    kpart[...] = jnp.zeros_like(kpart)

    def inner(i):
        span = pl.ds(pl.multiple_of(i * tile, tile), tile)
        kpart[...] += mult((vt_hi[i], vt_lo[i]), split(sr[0, span, :]))
    tile_loop(tiles, inner)
    go(copy(kpart.at[rows(mate % 2, half), :], kin.at[0], k_send.at[0], k_recv.at[0], mate, c))

    arrival = copy(vc, vc, vc_send.at[0], vc_recv.at[0], r, c)
    onward = copy(vc, vc, vc_send.at[0], vc_recv.at[0], mate, c)

    @pl.when(r != holder)
    def _():
        arrival.wait_recv()

        @pl.when(same)
        def _():
            onward.start()
    sends.append((onward, same))

    copy(kin.at[0], kin.at[0], k_send.at[0], k_recv.at[0], r, c).wait_recv()
    kpair[...] = kpart[rows(r % 2, half), :] + kin[0]
    for d in range(1, nrows // 2):
        go(copy(kpair, kin.at[d], k_send.at[d], k_recv.at[d], lax.rem(r + 2 * d, nrows), c))

    gather_scaled(1)
    klast[...] = jnp.zeros_like(klast)

    def inner_last(i):
        span = pl.ds(pl.multiple_of(i * tile, tile), tile)
        klast[...] += mult((vt_hi[i, hw:, :], vt_lo[i, hw:, :]), split(sr[1, span, :]))
    tile_loop(tiles, inner_last)
    for d in range(1, nrows):
        go(copy(klast, klin.at[d], kl_send.at[d], kl_recv.at[d], lax.rem(r + d, nrows), c))

    for d in range(1, nrows // 2):
        copy(kpair, kin.at[d], k_send.at[d], k_recv.at[d], r, c).wait_recv()
    summed = kpair[...]
    for d in range(1, nrows // 2):
        summed = summed + kin[d]
    mine_half = kfull.at[rows(r % 2, half), :]
    mine_half[...] = summed
    go(copy(mine_half, mine_half, kg_send.at[0], kg_recv.at[0], mate, c))

    everything = pl.ds(0, wide)
    vc_two = split(wide_of(vc, everything))

    def first(i):
        span = pl.ds(pl.multiple_of(i * tile, tile), tile)
        out_ref[span, :] = a_ref[span, :] - mult(split(wide_of(sr, span)), vc_two, NT)
    tile_loop(tiles, first)

    other_half = kfull.at[rows(mate % 2, half), :]
    copy(other_half, other_half, kg_send.at[0], kg_recv.at[0], r, c).wait_recv()
    k_two = split(kfull[...])
    k_turned = tuple(k[hw:, :] for k in k_two)
    vc_parts = [tuple(v[:, h * hw:(h + 1) * hw] for v in vc_two) for h in range(nh)]
    y_two = split(sc[0] - mult(vc_two, k_two))
    y_rest = sc[1] - mult(vc_parts[0], k_turned, NT)

    def second(i):
        span = pl.ds(pl.multiple_of(i * tile, tile), tile)
        out_ref[span, :] = out_ref[span, :] - mult(split(vr[0, span, :]), y_two, NT)
    tile_loop(tiles, second)
    mine = rows(c, blk)
    corr_ref[:, :hw] = sr[0, mine, :] - 0.5 * mult(split(wide_of(vr, mine)), k_two)
    corr_rest = mult(split(vr[0, mine, :]), k_turned, NT)

    for d in range(1, nrows):
        copy(klast, klin.at[d], kl_send.at[d], kl_recv.at[d], r, c).wait_recv()
    last = klast[...]
    for d in range(1, nrows):
        last = last + klin[d]
    last_two = split(last)
    y_last = split(y_rest - mult(vc_parts[1], last_two))

    def third(i):
        span = pl.ds(pl.multiple_of(i * tile, tile), tile)
        out_ref[span, :] = out_ref[span, :] - mult(split(vr[1, span, :]), y_last, NT)
    tile_loop(tiles, third)
    corr_ref[:, hw:] = sr[1, mine, :] - 0.5 * (corr_rest + mult(split(vr[1, mine, :]), last_two))

    pl.when(r == holder)(to_mate.wait_send)
    for desc, when in sends:
        if when is None:
            desc.wait_send()
        elif desc is onward:
            pl.when((r != holder) & when)(desc.wait_send)
        else:
            pl.when(when)(desc.wait_send)


def hand_out(held_ref, held_corr_ref, out_ref, corr_ref):
    out_ref[...] = held_ref[...]
    corr_ref[...] = held_corr_ref[...]


def per_device(nrows, ncols, matrix, panel, factor):
    total, wide = matrix.shape
    blk, width = panel.shape
    tile = 4 * blk
    tiles = total // tile
    group = ncols // (2 * nrows)
    lines = ncols // 2
    nh = 2
    hw = width // nh
    dma = pltpu.SemaphoreType.DMA
    vmem = pl.BlockSpec(memory_space=pltpu.VMEM)
    hbm = pl.BlockSpec(memory_space=pltpu.HBM)
    limit = 4 * (5 * total * wide + 4 * total * width + 4 * wide * width + 16 * width * width) + (8 << 20)
    held = pl.pallas_call(
        functools.partial(kernel, nrows, ncols, tile),
        out_shape=(jax.ShapeDtypeStruct(matrix.shape, F32), jax.ShapeDtypeStruct(panel.shape, F32)),
        in_specs=[hbm] * 3,
        out_specs=(vmem, vmem),
        scratch_shapes=[
            pltpu.VMEM((total, wide), F32),
            pltpu.VMEM((width, width), F32),
            pltpu.VMEM((nh, total, hw), F32),
            pltpu.VMEM((nh, wide, hw), F32),
            pltpu.VMEM((nh, total, hw), F32),
            pltpu.VMEM((nh, wide, hw), F32),
            pltpu.VMEM((nh, wide, hw), F32),
            pltpu.VMEM((nh, nrows, blk, hw), F32),
            pltpu.VMEM((width, hw), F32),
            pltpu.VMEM((nrows // 2, width // 2, hw), F32),
            pltpu.VMEM((width // 2, hw), F32),
            pltpu.VMEM((width, hw), F32),
            pltpu.VMEM((hw, hw), F32),
            pltpu.VMEM((nrows, hw, hw), F32),
            pltpu.VMEM((tiles, wide, tile), BF16),
            pltpu.VMEM((tiles, wide, tile), BF16),
            pltpu.VMEM((tiles, width, tile), BF16),
            pltpu.VMEM((tiles, width, tile), BF16),
            dma((nh + 2,)),
            dma((nh, lines)), dma((nh, lines)), dma((nh, lines)), dma((nh, lines)),
            dma((nh, nrows)), dma((nh, nrows)),
            dma((nh, lines)), dma((nh, nrows * group)), dma((nh,)),
            dma((nh, nrows * group)), dma((nh, nrows * group)),
            dma((nh, nrows)), dma((nh, nrows)),
            dma((nrows,)), dma((1,)), dma((nrows,)), dma((nrows,)), dma((1,)), dma((1,)),
            dma((nrows,)), dma((nrows,)),
        ],
        compiler_params=pltpu.CompilerParams(
            collective_id=0, has_side_effects=True, vmem_limit_bytes=limit),
    )(matrix, panel, factor)
    return pl.pallas_call(
        hand_out,
        out_shape=(jax.ShapeDtypeStruct(matrix.shape, F32), jax.ShapeDtypeStruct(panel.shape, F32)),
        in_specs=[vmem] * 2,
        out_specs=(vmem, vmem),
        compiler_params=pltpu.CompilerParams(vmem_limit_bytes=6 * total * wide * 4 + (1 << 20)),
    )(*held)


def solution(mesh):
    in_specs = (P("row", "col"), P(("row", "col"), None), P())
    out_specs = (P("row", "col"), P(("row", "col"), None))
    return jax.shard_map(
        functools.partial(per_device, mesh.shape["row"], mesh.shape["col"]),
        mesh=mesh, in_specs=in_specs, out_specs=out_specs, check_vma=False)
```

time: 47.6 us -> 42.9 us (0.901)
  the two profiles are of different devices: /device:TPU:5 before, /device:TPU:1 now
where the time goes in v1:
time: 42.9 us; the launch traced here: 42.7 us
  Pallas kernels  39.2 us (91%)
  local copies, waits for them, and re-layouts  2.82 us (7%)
  between operations  0.65 us (2%)
    pallas_call x1, Pallas kernels, per_device(): pl.pallas_call(functools.partial(kernel, nrows, ncols, tile), out_shape=(...  38.3 us
    unnamed x6, local copies, waits for them, and re-layouts  2.82 us

profile of v1, /device:TPU:1, one launch (start us, length us, event | category | flops | bytes accessed | tf_op | source)
XLA Modules:
  0.0 42.7 jit_solution(18255081537650976243)
XLA Ops:
  0.6 0.0 copy-start
  0.6 1.0 %copy-done = f32[512,256]{1,0:T(8,128)S(1)} copy-done((f32[512,256]{1,0:T(8,128)S(1)}, f32[512,256]{1,0:T(8,128)}, u32[]{:S(2)}) %copy-start) | copy-done | bytes 524312
  1.7 0.0 copy-start.1
  1.7 0.9 %copy-done.1 = f32[256,256]{1,0:T(8,128)S(1)} copy-done((f32[256,256]{1,0:T(8,128)S(1)}, f32[256,256]{1,0:T(8,128)}, u32[]{:S(2)}) %copy-start.1) | copy-done | bytes 262168
  2.6 0.0 copy-start.2
  2.6 0.8 %copy-done.2 = f32[64,256]{1,0:T(8,128)S(1)} copy-done((f32[64,256]{1,0:T(8,128)S(1)}, f32[64,256]{1,0:T(8,128)}, u32[]{:S(2)}) %copy-start.2) | copy-done | bytes 65560
  3.5 38.3 %shard_map.50 = (f32[512,256]{1,0:T(8,128)S(1)}, f32[64,256]{1,0:T(8,128)S(1)}) custom-call(f32[512,256]{1,0:T(8,128)S(1)} %copy-done, f32[64,256]{1,0:T(8,128)S(1)} %copy-done.2, f32[256,256]{1,0:T(8,128)S(1)} %copy-done.1), custom_call_target="tpu_custom_call" | custom-call | tf_op jit(solution)/shard_map/pallas_call | solution.py:360
  41.8 0.8 %shard_map.51 = (f32[512,256]{1,0:T(8,128)}, f32[64,256]{1,0:T(8,128)}) custom-call(f32[512,256]{1,0:T(8,128)S(1)} %get-tuple-element.4.held_ref, f32[64,256]{1,0:T(8,128)S(1)} %get-tuple-element.5.held_corr_ref), custom_call_target="tpu_custom_call" | custom-call | tf_op jit(solution)/shard_map/pallas_call | solution.py:396
Async XLA Ops:
  0.6 1.0 %copy-start = (f32[512,256]{1,0:T(8,128)S(1)}, f32[512,256]{1,0:T(8,128)}, u32[]{:S(2)}) copy-start(f32[512,256]{1,0:T(8,128)} %a_hbm.1) | copy-start | bytes 1572868
  1.7 0.9 %copy-start.1 = (f32[256,256]{1,0:T(8,128)S(1)}, f32[256,256]{1,0:T(8,128)}, u32[]{:S(2)}) copy-start(f32[256,256]{1,0:T(8,128)} %t_hbm.1) | copy-start | bytes 786436
  2.6 0.8 %copy-start.2 = (f32[64,256]{1,0:T(8,128)S(1)}, f32[64,256]{1,0:T(8,128)}, u32[]{:S(2)}) copy-start(f32[64,256]{1,0:T(8,128)} %panel_hbm.1) | copy-start | bytes 196612

commit v2 on v1

--- a/solution.py
+++ b/solution.py
@@ -392,7 +392,7 @@
         ],
         compiler_params=pltpu.CompilerParams(
             collective_id=0, has_side_effects=True, vmem_limit_bytes=limit),
-    )(matrix, panel, factor)
+    )(*(pltpu.with_memory_space_constraint(v, pltpu.HBM) for v in (matrix, panel, factor)))
     return pl.pallas_call(
         hand_out,
         out_shape=(jax.ShapeDtypeStruct(matrix.shape, F32), jax.ShapeDtypeStruct(panel.shape, F32)),

time: 42.9 us -> 40.1 us (0.935)
  local copies, waits for them, and re-layouts: 2.82 us -> 0 us
    unnamed x6 -> x0, local copies, waits for them, and re-layouts: 2.82 us -> none
where the time goes in v2:
time: 40.1 us; the launch traced here: 39.9 us
  Pallas kernels  39.3 us (98%)
  between operations  0.64 us (2%)
    pallas_call x1, Pallas kernels, per_device(): pl.pallas_call(functools.partial(kernel, nrows, ncols, tile), out_shape=(...  38.5 us
    pallas_call x1, Pallas kernels, per_device(): pl.pallas_call(hand_out, out_shape=(jax.ShapeDtypeStruct(matrix.shape, F3...  0.84 us

profile of v2, /device:TPU:1, one launch (start us, length us, event | category | flops | bytes accessed | tf_op | source)
XLA Modules:
  0.0 39.9 jit_solution(12562661449722512950)
XLA Ops:
  0.6 38.5 %shard_map.50 = (f32[512,256]{1,0:T(8,128)S(1)}, f32[64,256]{1,0:T(8,128)S(1)}) custom-call(f32[512,256]{1,0:T(8,128)} %a_hbm.1, f32[64,256]{1,0:T(8,128)} %panel_hbm.1, f32[256,256]{1,0:T(8,128)} %t_hbm.1), custom_call_target="tpu_custom_call" | custom-call | tf_op jit(solution)/shard_map/pallas_call | solution.py:360
  39.1 0.8 %shard_map.51 = (f32[512,256]{1,0:T(8,128)}, f32[64,256]{1,0:T(8,128)}) custom-call(f32[512,256]{1,0:T(8,128)S(1)} %get-tuple-element.4.held_ref, f32[64,256]{1,0:T(8,128)S(1)} %get-tuple-element.5.held_corr_ref), custom_call_target="tpu_custom_call" | custom-call | tf_op jit(solution)/shard_map/pallas_call | solution.py:396

commit v3 on v2

--- a/solution.py
+++ b/solution.py
@@ -36,11 +36,12 @@
 
 
 def kernel(nrows, ncols, tile, a_hbm, panel_hbm, t_hbm, out_ref, corr_ref,
-           a_ref, t_ref, vr, vc, sr, sc, q, qin, kpart, kin, kpair, kfull, klast, klin,
+           a_ref, t_ref, vr, vc, sr, sc, q, qin, kpart, kin, kpair, kside, kfull,
+           lpart, lin, lpair, lfull,
            at_hi, at_lo, vt_hi, vt_lo,
            local_sem, v_send, v_recv, vf_send, vf_recv, q_send, q_recv,
-           s_send, s_recv, sd_send, sf_send, sf_recv, sc_send, sc_recv,
-           vc_send, vc_recv, k_send, k_recv, kg_send, kg_recv, kl_send, kl_recv):
+           s_send, s_recv, sf_send, sf_recv, sc_send, sc_recv,
+           vc_send, vc_recv, k_send, k_recv, kg_send, kg_recv):
     r, c = lax.axis_index("row"), lax.axis_index("col")
     lines = ncols // 2
     group = ncols // (2 * nrows)
@@ -49,7 +50,6 @@
     nh, wide, hw = sc.shape
     blk, width = panel_hbm.shape
     tiles = total // tile
-    half = width // 2
     mate = r + 1 - 2 * (r % 2)
     far = lines // 2
 
@@ -77,6 +77,13 @@
             pl.when(when)(desc.start)
         sends.append((desc, when))
 
+    loads = [pltpu.make_async_copy(panel_hbm.at[:, pl.ds(h * hw, hw)], vr.at[h, rows(c, blk), :], local_sem.at[h])
+             for h in range(nh)]
+    loads.append(pltpu.make_async_copy(a_hbm, a_ref, local_sem.at[nh]))
+    loads.append(pltpu.make_async_copy(t_hbm, t_ref, local_sem.at[nh + 1]))
+    for load in loads:
+        load.start()
+
     opposite = peer(far)
     across = z * 2 + 1 - y
     target = z // group
@@ -91,6 +98,8 @@
     greet(r, opposite * 2 + 1 - y)
     for d in range(1, nrows):
         greet(lax.rem(r + d, nrows), c)
+    for d in range(1, nrows // 2):
+        greet(lax.rem(r + 2 * d, nrows), across)
     for g in range(group):
         line = r * group + g
 
@@ -99,28 +108,19 @@
             for d in range(1, nrows):
                 greet(lax.rem(r + d, nrows), line * 2 + y)
 
-        @pl.when(opposite == line)
-        def _():
-            for d in range(1, nrows):
-                greet(lax.rem(r + d, nrows), line * 2 + 1 - y)
-
-    loads = [pltpu.make_async_copy(panel_hbm.at[:, pl.ds(h * hw, hw)], vr.at[h, rows(c, blk), :], local_sem.at[h])
-             for h in range(nh)]
-    loads.append(pltpu.make_async_copy(a_hbm, a_ref, local_sem.at[nh]))
-    loads.append(pltpu.make_async_copy(t_hbm, t_ref, local_sem.at[nh + 1]))
-    for load in loads:
-        load.start()
     for h in range(nh):
         loads[h].wait()
-    pl.semaphore_wait(barrier, lines + nrows + jnp.where(target == r, 0, lines))
-
+    pl.semaphore_wait(barrier, lines + nrows + nrows // 2 - 1 + jnp.where(target == r, 0, lines - 1))
+
+    crossing = (False, False)
     order = [d for d in reversed(range(1, lines)) if d != far] + [far]
     for h in range(nh):
         own = vr.at[h, rows(c, blk), :]
         go(copy(own, own, v_send.at[h, z], v_recv.at[h, z], r, across))
         for d in order:
             go(copy(own, own, v_send.at[h, peer(d)], v_recv.at[h, z], r, peer(d) * 2 + y))
-        go(copy(own, own, vf_send.at[h, opposite], vf_recv.at[h, z], r, opposite * 2 + 1 - y))
+        if crossing[h]:
+            go(copy(own, own, vf_send.at[h, opposite], vf_recv.at[h, z], r, opposite * 2 + 1 - y))
 
     loads[nh].wait()
 
@@ -139,8 +139,8 @@
         return slot
 
     for h in range(nh):
-        for d in range(1, lines):
-            if d != far:
+        for d in sorted(range(1, lines), key=lambda d: d == far):
+            if d != far or not crossing[h]:
                 line = peer(d)
                 slot = arrived(h, line, y, v_recv)
                 go(copy(slot, slot, vf_send.at[h, line], vf_recv.at[h, line], r, across))
@@ -149,7 +149,7 @@
         for e in range(tiles):
             for d in (2 * e, 2 * e + 1):
                 line = peer(d)
-                if d == far:
+                if d == far and crossing[h]:
                     arrived(h, line, y, v_recv)
                 arrived(h, line, 1 - y, vf_recv if d else v_recv)
             i = peer(2 * e) // 2
@@ -189,27 +189,25 @@
         slot = sr.at[h, rows(place, blk), :]
         for d in order:
             go(copy(mine, slot, s_send.at[h, peer(d)], s_recv.at[h, here], target, peer(d) * 2 + y))
-        go(copy(mine, slot, sd_send.at[h], sf_recv.at[h, here], target, opposite * 2 + 1 - y))
-        for d in range(1, nrows):
-            go(copy(mine, mine, sc_send.at[h, d], sc_recv.at[h, d], lax.rem(r + d, nrows), c))
+        for d in range(1, nrows // 2):
+            go(copy(mine, mine, sc_send.at[h, 2 * d], sc_recv.at[h, 2 * d], lax.rem(r + 2 * d, nrows), c))
+        go(copy(mine, mine, sc_send.at[h, 1], sc_recv.at[h, 1], mate, c))
 
     holder = c * nrows // ncols
     first_block = lax.rem(c * nrows, ncols)
     v_slice = vr.at[:, rows(first_block // nrows, wide), :]
     same = r % 2 == holder % 2
-    for d in range(1, nrows // 2):
-        go(copy(v_slice, vc, vc_send.at[d], vc_recv.at[0], lax.rem(r + 2 * d, nrows), c), r == holder)
-    to_mate = copy(v_slice, vc, vc_send.at[0], vc_recv.at[0], mate, c)
-
-    @pl.when(r == holder)
-    def _():
-        to_mate.start()
-        vc[...] = v_slice[...]
+    def from_mate(h):
+        for d in range(nrows // 2):
+            slot = sc.at[h, rows(lax.rem(mate - 2 * d + nrows, nrows), blk), :]
+            copy(slot, slot, sc_send.at[h, 2 * d + 1], sc_recv.at[h, 2 * d + 1], r, c).wait_recv()
 
     def forward_scaled(h):
-        for d in range(1, nrows):
-            slot = sc.at[h, rows(lax.rem(r - d + nrows, nrows), blk), :]
-            copy(slot, slot, sc_send.at[h, d], sc_recv.at[h, d], r, c).wait_recv()
+        for d in range(1, nrows // 2):
+            slot = sc.at[h, rows(lax.rem(r - 2 * d + nrows, nrows), blk), :]
+            copy(slot, slot, sc_send.at[h, 2 * d], sc_recv.at[h, 2 * d], r, c).wait_recv()
+            go(copy(slot, slot, sc_send.at[h, 2 * d + 1], sc_recv.at[h, 2 * d + 1], mate, c))
+        pl.when(target == r)(functools.partial(from_mate, h))
         for g in range(group):
             line = r * group + g
             for d in range(nrows):
@@ -229,11 +227,8 @@
                 @pl.when(z != line)
                 def _():
                     came.wait_recv()
-
-                    @pl.when(opposite != line)
-                    def _():
-                        passed.start()
-                sends.append((passed, opposite != line))
+                    passed.start()
+                sends.append((passed, None))
 
     def gather_scaled(h):
         for g in range(group):
@@ -243,17 +238,64 @@
                 slot = sr.at[h, rows(lax.rem((line * 2 + 1 - y) * nrows + j, ncols), blk), :]
                 copy(slot, slot, sf_send.at[h, at], sf_recv.at[h, at], r, c).wait_recv()
 
-    for h in range(nh):
-        forward_scaled(h)
+    def small(h, part, base):
+        part[...] = jnp.zeros_like(part)
+        for g in range(group):
+            start = lax.rem(((r * group + g) * 2 + y) * nrows, ncols) * blk // tile
+            for i in range(nrows * blk // tile):
+                at = start + i
+                part[...] += mult((vt_hi[at, base:, :], vt_lo[at, base:, :]), split(sr[h, rows(at, tile), :]))
+
+    def pair_up(h, part, room, pair):
+        size = pair.shape[0]
+        go(copy(part.at[rows(mate % 2, size), :], room.at[0], k_send.at[h, 0], k_recv.at[h, 0], mate, c))
+        copy(room.at[0], room.at[0], k_send.at[h, 0], k_recv.at[h, 0], r, c).wait_recv()
+        pair[...] = part[rows(r % 2, size), :] + room[0]
+
+    def spread(h, room, pair, slots):
+        for i in slots:
+            row, col = lax.rem(r + i // 2 * 2, nrows), across if i % 2 else c
+            go(copy(pair, room.at[i], k_send.at[h, i], k_recv.at[h, i], row, col))
+
+    def collect(h, room, pair, slots):
+        for i in slots:
+            copy(pair, room.at[i], k_send.at[h, i], k_recv.at[h, i], r, c).wait_recv()
+        summed = pair[...]
+        for i in slots:
+            summed = summed + room[i]
+        return summed
+
+    def finish_half(h, full, summed):
+        mine = full.at[rows(r % 2, summed.shape[0]), :]
+        mine[...] = summed
+        go(copy(mine, mine, kg_send.at[h], kg_recv.at[h], mate, c))
+
+    def completed(h, pair, full):
+        other = full.at[rows(mate % 2, pair.shape[0]), :]
+        copy(other, other, kg_send.at[h], kg_recv.at[h], r, c).wait_recv()
+        return split(full[...])
+
+    forward_scaled(0)
+    small(0, kpart, 0)
+    pair_up(0, kpart, kin, kpair)
+    spread(0, kin, kpair, range(2, nrows, 2))
+    forward_scaled(1)
+    small(1, lpart, hw)
+    pair_up(1, lpart, lin, lpair)
+    spread(1, lin, lpair, range(1, nrows))
+    for d in range(1, nrows // 2):
+        go(copy(v_slice, vc, vc_send.at[d], vc_recv.at[0], lax.rem(r + 2 * d, nrows), c), r == holder)
+    to_mate = copy(v_slice, vc, vc_send.at[0], vc_recv.at[0], mate, c)
+
+    @pl.when(r == holder)
+    def _():
+        to_mate.start()
+        vc[...] = v_slice[...]
+
 
     gather_scaled(0)
-    kpart[...] = jnp.zeros_like(kpart)
-
-    def inner(i):
-        span = pl.ds(pl.multiple_of(i * tile, tile), tile)
-        kpart[...] += mult((vt_hi[i], vt_lo[i]), split(sr[0, span, :]))
-    tile_loop(tiles, inner)
-    go(copy(kpart.at[rows(mate % 2, half), :], kin.at[0], k_send.at[0], k_recv.at[0], mate, c))
+    kside[...] = collect(0, kin, kpair, range(2, nrows, 2))
+    spread(0, kin, kside, (1,))
 
     arrival = copy(vc, vc, vc_send.at[0], vc_recv.at[0], r, c)
     onward = copy(vc, vc, vc_send.at[0], vc_recv.at[0], mate, c)
@@ -266,30 +308,7 @@
         def _():
             onward.start()
     sends.append((onward, same))
-
-    copy(kin.at[0], kin.at[0], k_send.at[0], k_recv.at[0], r, c).wait_recv()
-    kpair[...] = kpart[rows(r % 2, half), :] + kin[0]
-    for d in range(1, nrows // 2):
-        go(copy(kpair, kin.at[d], k_send.at[d], k_recv.at[d], lax.rem(r + 2 * d, nrows), c))
-
     gather_scaled(1)
-    klast[...] = jnp.zeros_like(klast)
-
-    def inner_last(i):
-        span = pl.ds(pl.multiple_of(i * tile, tile), tile)
-        klast[...] += mult((vt_hi[i, hw:, :], vt_lo[i, hw:, :]), split(sr[1, span, :]))
-    tile_loop(tiles, inner_last)
-    for d in range(1, nrows):
-        go(copy(klast, klin.at[d], kl_send.at[d], kl_recv.at[d], lax.rem(r + d, nrows), c))
-
-    for d in range(1, nrows // 2):
-        copy(kpair, kin.at[d], k_send.at[d], k_recv.at[d], r, c).wait_recv()
-    summed = kpair[...]
-    for d in range(1, nrows // 2):
-        summed = summed + kin[d]
-    mine_half = kfull.at[rows(r % 2, half), :]
-    mine_half[...] = summed
-    go(copy(mine_half, mine_half, kg_send.at[0], kg_recv.at[0], mate, c))
 
     everything = pl.ds(0, wide)
     vc_two = split(wide_of(vc, everything))
@@ -299,11 +318,13 @@
         out_ref[span, :] = a_ref[span, :] - mult(split(wide_of(sr, span)), vc_two, NT)
     tile_loop(tiles, first)
 
-    other_half = kfull.at[rows(mate % 2, half), :]
-    copy(other_half, other_half, kg_send.at[0], kg_recv.at[0], r, c).wait_recv()
-    k_two = split(kfull[...])
+    finish_half(1, lfull, collect(1, lin, lpair, range(1, nrows)))
+    finish_half(0, kfull, collect(0, kin, kside, (1,)))
+    k_two = completed(0, kpair, kfull)
     k_turned = tuple(k[hw:, :] for k in k_two)
     vc_parts = [tuple(v[:, h * hw:(h + 1) * hw] for v in vc_two) for h in range(nh)]
+    for h in range(nh):
+        pl.when(target != r)(functools.partial(from_mate, h))
     y_two = split(sc[0] - mult(vc_two, k_two))
     y_rest = sc[1] - mult(vc_parts[0], k_turned, NT)
 
@@ -315,12 +336,7 @@
     corr_ref[:, :hw] = sr[0, mine, :] - 0.5 * mult(split(wide_of(vr, mine)), k_two)
     corr_rest = mult(split(vr[0, mine, :]), k_turned, NT)
 
-    for d in range(1, nrows):
-        copy(klast, klin.at[d], kl_send.at[d], kl_recv.at[d], r, c).wait_recv()
-    last = klast[...]
-    for d in range(1, nrows):
-        last = last + klin[d]
-    last_two = split(last)
+    last_two = completed(1, lpair, lfull)
     y_last = split(y_rest - mult(vc_parts[1], last_two))
 
     def third(i):
@@ -372,11 +388,14 @@
             pltpu.VMEM((nh, wide, hw), F32),
             pltpu.VMEM((nh, nrows, blk, hw), F32),
             pltpu.VMEM((width, hw), F32),
-            pltpu.VMEM((nrows // 2, width // 2, hw), F32),
+            pltpu.VMEM((nrows, width // 2, hw), F32),
+            pltpu.VMEM((width // 2, hw), F32),
             pltpu.VMEM((width // 2, hw), F32),
             pltpu.VMEM((width, hw), F32),
             pltpu.VMEM((hw, hw), F32),
-            pltpu.VMEM((nrows, hw, hw), F32),
+            pltpu.VMEM((nrows, hw // 2, hw), F32),
+            pltpu.VMEM((hw // 2, hw), F32),
+            pltpu.VMEM((hw, hw), F32),
             pltpu.VMEM((tiles, wide, tile), BF16),
             pltpu.VMEM((tiles, wide, tile), BF16),
             pltpu.VMEM((tiles, width, tile), BF16),
@@ -384,11 +403,10 @@
             dma((nh + 2,)),
             dma((nh, lines)), dma((nh, lines)), dma((nh, lines)), dma((nh, lines)),
             dma((nh, nrows)), dma((nh, nrows)),
-            dma((nh, lines)), dma((nh, nrows * group)), dma((nh,)),
+            dma((nh, lines)), dma((nh, nrows * group)),
             dma((nh, nrows * group)), dma((nh, nrows * group)),
             dma((nh, nrows)), dma((nh, nrows)),
-            dma((nrows,)), dma((1,)), dma((nrows,)), dma((nrows,)), dma((1,)), dma((1,)),
-            dma((nrows,)), dma((nrows,)),
+            dma((nrows,)), dma((1,)), dma((nh, nrows)), dma((nh, nrows)), dma((nh,)), dma((nh,)),
         ],
         compiler_params=pltpu.CompilerParams(
             collective_id=0, has_side_effects=True, vmem_limit_bytes=limit),

time: 40.1 us -> 37.6 us (0.938)
  the two profiles are of different devices: /device:TPU:1 before, /device:TPU:7 now
where the time goes in v3:
time: 37.6 us; the launch traced here: 37.4 us
  Pallas kernels  36.8 us (98%)
  between operations  0.64 us (2%)
    pallas_call x1, Pallas kernels, per_device(): pl.pallas_call(functools.partial(kernel, nrows, ncols, tile), out_shape=(...  35.9 us
    pallas_call x1, Pallas kernels, per_device(): pl.pallas_call(hand_out, out_shape=(jax.ShapeDtypeStruct(matrix.shape, F3...  0.84 us

profile of v3, /device:TPU:7, one launch (start us, length us, event | category | flops | bytes accessed | tf_op | source)
XLA Modules:
  0.0 37.4 jit_solution(4893030092462164160)
XLA Ops:
  0.6 35.9 %shard_map.50 = (f32[512,256]{1,0:T(8,128)S(1)}, f32[64,256]{1,0:T(8,128)S(1)}) custom-call(f32[512,256]{1,0:T(8,128)} %a_hbm.1, f32[64,256]{1,0:T(8,128)} %panel_hbm.1, f32[256,256]{1,0:T(8,128)} %t_hbm.1), custom_call_target="tpu_custom_call" | custom-call | tf_op jit(solution)/shard_map/pallas_call | solution.py:376
  36.6 0.8 %shard_map.51 = (f32[512,256]{1,0:T(8,128)}, f32[64,256]{1,0:T(8,128)}) custom-call(f32[512,256]{1,0:T(8,128)S(1)} %get-tuple-element.4.held_ref, f32[64,256]{1,0:T(8,128)S(1)} %get-tuple-element.5.held_corr_ref), custom_call_target="tpu_custom_call" | custom-call | tf_op jit(solution)/shard_map/pallas_call | solution.py:414

commit v4 on v3

--- a/solution.py
+++ b/solution.py
@@ -51,7 +51,6 @@
     blk, width = panel_hbm.shape
     tiles = total // tile
     mate = r + 1 - 2 * (r % 2)
-    far = lines // 2
 
     def rows(index, size):
         return pl.ds(pl.multiple_of(index * size, size), size)
@@ -70,6 +69,14 @@
 
     sends = []
 
+    def drain():
+        for desc, when in sends:
+            if when is None:
+                desc.wait_send()
+            else:
+                pl.when(when)(desc.wait_send)
+        sends.clear()
+
     def go(desc, when=None):
         if when is None:
             desc.start()
@@ -84,7 +91,6 @@
     for load in loads:
         load.start()
 
-    opposite = peer(far)
     across = z * 2 + 1 - y
     target = z // group
     barrier = pltpu.get_barrier_semaphore()
@@ -95,7 +101,6 @@
     for d in range(1, lines):
         greet(r, peer(d) * 2 + y)
     greet(r, across)
-    greet(r, opposite * 2 + 1 - y)
     for d in range(1, nrows):
         greet(lax.rem(r + d, nrows), c)
     for d in range(1, nrows // 2):
@@ -110,17 +115,14 @@
 
     for h in range(nh):
         loads[h].wait()
-    pl.semaphore_wait(barrier, lines + nrows + nrows // 2 - 1 + jnp.where(target == r, 0, lines - 1))
-
-    crossing = (False, False)
-    order = [d for d in reversed(range(1, lines)) if d != far] + [far]
+    pl.semaphore_wait(barrier, lines + nrows + nrows // 2 - 2 + jnp.where(target == r, 0, lines - 1))
+
+    order = list(range(1, lines))
     for h in range(nh):
         own = vr.at[h, rows(c, blk), :]
         go(copy(own, own, v_send.at[h, z], v_recv.at[h, z], r, across))
         for d in order:
             go(copy(own, own, v_send.at[h, peer(d)], v_recv.at[h, z], r, peer(d) * 2 + y))
-        if crossing[h]:
-            go(copy(own, own, vf_send.at[h, opposite], vf_recv.at[h, z], r, opposite * 2 + 1 - y))
 
     loads[nh].wait()
 
@@ -139,19 +141,15 @@
         return slot
 
     for h in range(nh):
-        for d in sorted(range(1, lines), key=lambda d: d == far):
-            if d != far or not crossing[h]:
-                line = peer(d)
-                slot = arrived(h, line, y, v_recv)
-                go(copy(slot, slot, vf_send.at[h, line], vf_recv.at[h, line], r, across))
+        for d in range(1, lines):
+            line = peer(d)
+            slot = arrived(h, line, y, v_recv)
+            go(copy(slot, slot, vf_send.at[h, line], vf_recv.at[h, line], r, across))
 
     def reduce_product(h):
         for e in range(tiles):
             for d in (2 * e, 2 * e + 1):
-                line = peer(d)
-                if d == far and crossing[h]:
-                    arrived(h, line, y, v_recv)
-                arrived(h, line, 1 - y, vf_recv if d else v_recv)
+                arrived(h, peer(d), 1 - y, vf_recv if d else v_recv)
             i = peer(2 * e) // 2
             part = mult((at_hi[i], at_lo[i]), split(vr[h, rows(i, tile), :]))
             q[h] = part if e == 0 else q[h] + part
@@ -275,6 +273,8 @@
         copy(other, other, kg_send.at[h], kg_recv.at[h], r, c).wait_recv()
         return split(full[...])
 
+    older = sends[:]
+    sends.clear()
     forward_scaled(0)
     small(0, kpart, 0)
     pair_up(0, kpart, kin, kpair)
@@ -291,8 +291,13 @@
     def _():
         to_mate.start()
         vc[...] = v_slice[...]
-
-
+    sends.append((to_mate, r == holder))
+
+
+    newer = sends[:]
+    sends[:] = older
+    drain()
+    sends[:] = newer
     gather_scaled(0)
     kside[...] = collect(0, kin, kpair, range(2, nrows, 2))
     spread(0, kin, kside, (1,))
@@ -307,7 +312,7 @@
         @pl.when(same)
         def _():
             onward.start()
-    sends.append((onward, same))
+    sends.append((onward, (r != holder) & same))
     gather_scaled(1)
 
     everything = pl.ds(0, wide)
@@ -320,39 +325,22 @@
 
     finish_half(1, lfull, collect(1, lin, lpair, range(1, nrows)))
     finish_half(0, kfull, collect(0, kin, kside, (1,)))
-    k_two = completed(0, kpair, kfull)
-    k_turned = tuple(k[hw:, :] for k in k_two)
-    vc_parts = [tuple(v[:, h * hw:(h + 1) * hw] for v in vc_two) for h in range(nh)]
     for h in range(nh):
         pl.when(target != r)(functools.partial(from_mate, h))
-    y_two = split(sc[0] - mult(vc_two, k_two))
-    y_rest = sc[1] - mult(vc_parts[0], k_turned, NT)
+    completed(0, kpair, kfull)
+    completed(1, lpair, lfull)
+    left = kfull[...]
+    right = jnp.concatenate([left[hw:, :].T, lfull[...]], axis=0)
+    k_two = split(jnp.concatenate([left, right], axis=1))
+    y_two = split(wide_of(sc, everything) - mult(vc_two, k_two))
 
     def second(i):
         span = pl.ds(pl.multiple_of(i * tile, tile), tile)
-        out_ref[span, :] = out_ref[span, :] - mult(split(vr[0, span, :]), y_two, NT)
+        out_ref[span, :] = out_ref[span, :] - mult(split(wide_of(vr, span)), y_two, NT)
     tile_loop(tiles, second)
     mine = rows(c, blk)
-    corr_ref[:, :hw] = sr[0, mine, :] - 0.5 * mult(split(wide_of(vr, mine)), k_two)
-    corr_rest = mult(split(vr[0, mine, :]), k_turned, NT)
-
-    last_two = completed(1, lpair, lfull)
-    y_last = split(y_rest - mult(vc_parts[1], last_two))
-
-    def third(i):
-        span = pl.ds(pl.multiple_of(i * tile, tile), tile)
-        out_ref[span, :] = out_ref[span, :] - mult(split(vr[1, span, :]), y_last, NT)
-    tile_loop(tiles, third)
-    corr_ref[:, hw:] = sr[1, mine, :] - 0.5 * (corr_rest + mult(split(vr[1, mine, :]), last_two))
-
-    pl.when(r == holder)(to_mate.wait_send)
-    for desc, when in sends:
-        if when is None:
-            desc.wait_send()
-        elif desc is onward:
-            pl.when((r != holder) & when)(desc.wait_send)
-        else:
-            pl.when(when)(desc.wait_send)
+    corr_ref[...] = wide_of(sr, mine) - 0.5 * mult(split(wide_of(vr, mine)), k_two)
+    drain()
 
 
 def hand_out(held_ref, held_corr_ref, out_ref, corr_ref):

time: 37.6 us -> 36.4 us (0.968)
  the two profiles are of different devices: /device:TPU:7 before, /device:TPU:1 now
where the time goes in v4:
time: 36.4 us; the launch traced here: 35.8 us
  Pallas kernels  35.2 us (97%)
  between operations  0.64 us (2%)
    pallas_call x1, Pallas kernels, per_device(): pl.pallas_call(functools.partial(kernel, nrows, ncols, tile), out_shape=(...  34.3 us
    pallas_call x1, Pallas kernels, per_device(): pl.pallas_call(hand_out, out_shape=(jax.ShapeDtypeStruct(matrix.shape, F3...  0.84 us

profile of v4, /device:TPU:1, one launch (start us, length us, event | category | flops | bytes accessed | tf_op | source)
XLA Modules:
  0.0 35.8 jit_solution(1952365737199855832)
XLA Ops:
  0.6 34.3 %shard_map.50 = (f32[512,256]{1,0:T(8,128)S(1)}, f32[64,256]{1,0:T(8,128)S(1)}) custom-call(f32[512,256]{1,0:T(8,128)} %a_hbm.1, f32[64,256]{1,0:T(8,128)} %panel_hbm.1, f32[256,256]{1,0:T(8,128)} %t_hbm.1), custom_call_target="tpu_custom_call" | custom-call | tf_op jit(solution)/shard_map/pallas_call | solution.py:364
  35.0 0.8 %shard_map.51 = (f32[512,256]{1,0:T(8,128)}, f32[64,256]{1,0:T(8,128)}) custom-call(f32[512,256]{1,0:T(8,128)S(1)} %get-tuple-element.4.held_ref, f32[64,256]{1,0:T(8,128)S(1)} %get-tuple-element.5.held_corr_ref), custom_call_target="tpu_custom_call" | custom-call | tf_op jit(solution)/shard_map/pallas_call | solution.py:402

commit v5 on v4

--- a/solution.py
+++ b/solution.py
@@ -35,7 +35,7 @@
         pl.loop(0, count)(body)
 
 
-def kernel(nrows, ncols, tile, a_hbm, panel_hbm, t_hbm, out_ref, corr_ref,
+def kernel(nrows, ncols, tile, a_hbm, panel_hbm, t_hbm, out_ref, corr_ref, v_hi, v_lo, y_hi, y_lo,
            a_ref, t_ref, vr, vc, sr, sc, q, qin, kpart, kin, kpair, kside, kfull,
            lpart, lin, lpair, lfull,
            at_hi, at_lo, vt_hi, vt_lo,
@@ -103,19 +103,9 @@
     greet(r, across)
     for d in range(1, nrows):
         greet(lax.rem(r + d, nrows), c)
-    for d in range(1, nrows // 2):
-        greet(lax.rem(r + 2 * d, nrows), across)
-    for g in range(group):
-        line = r * group + g
-
-        @pl.when(z != line)
-        def _():
-            for d in range(1, nrows):
-                greet(lax.rem(r + d, nrows), line * 2 + y)
-
     for h in range(nh):
         loads[h].wait()
-    pl.semaphore_wait(barrier, lines + nrows + nrows // 2 - 2 + jnp.where(target == r, 0, lines - 1))
+    pl.semaphore_wait(barrier, lines + nrows - 1)
 
     order = list(range(1, lines))
     for h in range(nh):
@@ -145,6 +135,29 @@
             line = peer(d)
             slot = arrived(h, line, y, v_recv)
             go(copy(slot, slot, vf_send.at[h, line], vf_recv.at[h, line], r, across))
+
+    holder = c * nrows // ncols
+    first_block = lax.rem(c * nrows, ncols)
+    same = r % 2 == holder % 2
+
+    def hand_panel(h):
+        held = vr.at[h, rows(first_block // nrows, wide), :]
+        kept = vc.at[h]
+        for d in range(1, nrows // 2):
+            go(copy(held, kept, vc_send.at[h, d], vc_recv.at[h], lax.rem(r + 2 * d, nrows), c), r == holder)
+        go(copy(held, kept, vc_send.at[h, 0], vc_recv.at[h], mate, c), r == holder)
+
+        @pl.when(r == holder)
+        def _():
+            kept[...] = held[...]
+
+    def pass_panel(h):
+        kept = vc.at[h]
+
+        @pl.when(r != holder)
+        def _():
+            copy(kept, kept, vc_send.at[h, 0], vc_recv.at[h], r, c).wait_recv()
+        go(copy(kept, kept, vc_send.at[h, 0], vc_recv.at[h], mate, c), (r != holder) & same)
 
     def reduce_product(h):
         for e in range(tiles):
@@ -157,12 +170,15 @@
             other = lax.rem(r + d, nrows)
             go(copy(q.at[h, rows(other, blk), :], qin.at[h, d], q_send.at[h, d], q_recv.at[h, d], other, c))
 
-    for h in range(nh):
-        reduce_product(h)
+    reduce_product(0)
+    hand_panel(0)
+    reduce_product(1)
 
     def turn(i):
         span = pl.ds(pl.multiple_of(i * tile, tile), tile)
-        high, low = split(mult(tt_two, split(wide_of(vr, span)), NT))
+        v_two = split(wide_of(vr, span))
+        v_hi[span, :], v_lo[span, :] = v_two
+        high, low = split(mult(tt_two, v_two, NT))
         vt_hi[i] = high
         vt_lo[i] = low
     tile_loop(tiles, turn)
@@ -191,10 +207,6 @@
             go(copy(mine, mine, sc_send.at[h, 2 * d], sc_recv.at[h, 2 * d], lax.rem(r + 2 * d, nrows), c))
         go(copy(mine, mine, sc_send.at[h, 1], sc_recv.at[h, 1], mate, c))
 
-    holder = c * nrows // ncols
-    first_block = lax.rem(c * nrows, ncols)
-    v_slice = vr.at[:, rows(first_block // nrows, wide), :]
-    same = r % 2 == holder % 2
     def from_mate(h):
         for d in range(nrows // 2):
             slot = sc.at[h, rows(lax.rem(mate - 2 * d + nrows, nrows), blk), :]
@@ -273,6 +285,7 @@
         copy(other, other, kg_send.at[h], kg_recv.at[h], r, c).wait_recv()
         return split(full[...])
 
+    hand_panel(1)
     older = sends[:]
     sends.clear()
     forward_scaled(0)
@@ -283,36 +296,18 @@
     small(1, lpart, hw)
     pair_up(1, lpart, lin, lpair)
     spread(1, lin, lpair, range(1, nrows))
-    for d in range(1, nrows // 2):
-        go(copy(v_slice, vc, vc_send.at[d], vc_recv.at[0], lax.rem(r + 2 * d, nrows), c), r == holder)
-    to_mate = copy(v_slice, vc, vc_send.at[0], vc_recv.at[0], mate, c)
-
-    @pl.when(r == holder)
-    def _():
-        to_mate.start()
-        vc[...] = v_slice[...]
-    sends.append((to_mate, r == holder))
+    pass_panel(0)
 
 
     newer = sends[:]
     sends[:] = older
     drain()
     sends[:] = newer
-    gather_scaled(0)
     kside[...] = collect(0, kin, kpair, range(2, nrows, 2))
     spread(0, kin, kside, (1,))
-
-    arrival = copy(vc, vc, vc_send.at[0], vc_recv.at[0], r, c)
-    onward = copy(vc, vc, vc_send.at[0], vc_recv.at[0], mate, c)
-
-    @pl.when(r != holder)
-    def _():
-        arrival.wait_recv()
-
-        @pl.when(same)
-        def _():
-            onward.start()
-    sends.append((onward, (r != holder) & same))
+    gather_scaled(0)
+
+    pass_panel(1)
     gather_scaled(1)
 
     everything = pl.ds(0, wide)
@@ -332,20 +327,23 @@
     left = kfull[...]
     right = jnp.concatenate([left[hw:, :].T, lfull[...]], axis=0)
     k_two = split(jnp.concatenate([left, right], axis=1))
-    y_two = split(wide_of(sc, everything) - mult(vc_two, k_two))
-
-    def second(i):
-        span = pl.ds(pl.multiple_of(i * tile, tile), tile)
-        out_ref[span, :] = out_ref[span, :] - mult(split(wide_of(vr, span)), y_two, NT)
-    tile_loop(tiles, second)
+    y_hi[...], y_lo[...] = split(wide_of(sc, everything) - mult(vc_two, k_two))
     mine = rows(c, blk)
-    corr_ref[...] = wide_of(sr, mine) - 0.5 * mult(split(wide_of(vr, mine)), k_two)
+    corr_ref[...] = wide_of(sr, mine) - 0.5 * mult((v_hi[mine, :], v_lo[mine, :]), k_two)
     drain()
 
 
-def hand_out(held_ref, held_corr_ref, out_ref, corr_ref):
-    out_ref[...] = held_ref[...]
-    corr_ref[...] = held_corr_ref[...]
+def hand_out(tile, held_ref, held_corr_ref, v_hi, v_lo, y_hi, y_lo, out_hbm, corr_hbm, stage, sem):
+    tiles = held_ref.shape[0] // tile
+    copies = [pltpu.make_async_copy(held_corr_ref, corr_hbm, sem.at[tiles])]
+    copies[0].start()
+    for i in range(tiles):
+        span = pl.ds(i * tile, tile)
+        stage[span, :] = held_ref[span, :] - mult((v_hi[span, :], v_lo[span, :]), (y_hi[...], y_lo[...]), NT)
+        copies.append(pltpu.make_async_copy(stage.at[span, :], out_hbm.at[span, :], sem.at[i]))
+        copies[-1].start()
+    for copy in copies:
+        copy.wait()
 
 
 def per_device(nrows, ncols, matrix, panel, factor):
@@ -363,9 +361,11 @@
     limit = 4 * (5 * total * wide + 4 * total * width + 4 * wide * width + 16 * width * width) + (8 << 20)
     held = pl.pallas_call(
         functools.partial(kernel, nrows, ncols, tile),
-        out_shape=(jax.ShapeDtypeStruct(matrix.shape, F32), jax.ShapeDtypeStruct(panel.shape, F32)),
+        out_shape=(jax.ShapeDtypeStruct(matrix.shape, F32), jax.ShapeDtypeStruct(panel.shape, F32),
+                   jax.ShapeDtypeStruct((total, width), BF16), jax.ShapeDtypeStruct((total, width), BF16),
+                   jax.ShapeDtypeStruct((wide, width), BF16), jax.ShapeDtypeStruct((wide, width), BF16)),
         in_specs=[hbm] * 3,
-        out_specs=(vmem, vmem),
+        out_specs=(vmem,) * 6,
         scratch_shapes=[
             pltpu.VMEM((total, wide), F32),
             pltpu.VMEM((width, width), F32),
@@ -394,17 +394,18 @@
             dma((nh, lines)), dma((nh, nrows * group)),
             dma((nh, nrows * group)), dma((nh, nrows * group)),
             dma((nh, nrows)), dma((nh, nrows)),
-            dma((nrows,)), dma((1,)), dma((nh, nrows)), dma((nh, nrows)), dma((nh,)), dma((nh,)),
+            dma((nh, nrows)), dma((nh,)), dma((nh, nrows)), dma((nh, nrows)), dma((nh,)), dma((nh,)),
         ],
         compiler_params=pltpu.CompilerParams(
             collective_id=0, has_side_effects=True, vmem_limit_bytes=limit),
     )(*(pltpu.with_memory_space_constraint(v, pltpu.HBM) for v in (matrix, panel, factor)))
     return pl.pallas_call(
-        hand_out,
+        functools.partial(hand_out, tile),
         out_shape=(jax.ShapeDtypeStruct(matrix.shape, F32), jax.ShapeDtypeStruct(panel.shape, F32)),
-        in_specs=[vmem] * 2,
-        out_specs=(vmem, vmem),
-        compiler_params=pltpu.CompilerParams(vmem_limit_bytes=6 * total * wide * 4 + (1 << 20)),
+        in_specs=[vmem] * 6,
+        out_specs=(hbm, hbm),
+        scratch_shapes=[pltpu.VMEM((total, wide), F32), dma((tiles + 1,))],
+        compiler_params=pltpu.CompilerParams(vmem_limit_bytes=8 * total * wide * 4 + (4 << 20)),
     )(*held)
 
 

time: 36.4 us -> 35.4 us (0.973); the launches traced: 35.8 us -> 35.2 us
  Pallas kernels: 35.2 us -> 34.6 us
    pallas_call x1, Pallas kernels: 34.3 us -> 33.4 us  [per_device(): pl.pallas_call(functools.partial(kernel, nrows, ncols, tile), out_shape=(...]
    pallas_call x1, Pallas kernels: 0.84 us -> 1.22 us  [per_device(): pl.pallas_call(functools.partial(hand_out, tile), out_shape=(jax.ShapeDty...]
where the time goes in v5:
time: 35.4 us; the launch traced here: 35.2 us
  Pallas kernels  34.6 us (98%)
  between operations  0.64 us (2%)
    pallas_call x1, Pallas kernels, per_device(): pl.pallas_call(functools.partial(kernel, nrows, ncols, tile), out_shape=(...  33.4 us
    pallas_call x1, Pallas kernels, per_device(): pl.pallas_call(functools.partial(hand_out, tile), out_shape=(jax.ShapeDty...  1.22 us

profile of v5, /device:TPU:1, one launch (start us, length us, event | category | flops | bytes accessed | tf_op | source)
XLA Modules:
  0.0 35.2 jit_solution(16596924631800973937)
XLA Ops:
  0.6 33.4 %shard_map.50 = (f32[512,256]{1,0:T(8,128)S(1)}, f32[64,256]{1,0:T(8,128)S(1)}, bf16[512,256]{1,0:T(8,128)(2,1)S(1)}, bf16[512,256]{1,0:T(8,128)(2,1)S(1)}, bf16...) custom-call(f32[512,256]{1,0:T(8,128)} %a_hbm.1, f32[64,256]{1,0:T(8,128)} %panel_hbm.1, f32[256,256]{1,0:T(8,128)} %t_hbm.1), custom_call_target="tpu_custom_call" | custom-call | tf_op jit(solution)/shard_map/pallas_call | solution.py:362
  34.0 1.2 %shard_map.51 = (f32[512,256]{1,0:T(8,128)}, f32[64,256]{1,0:T(8,128)}) custom-call(f32[512,256]{1,0:T(8,128)S(1)} %get-tuple-element.8.held_ref, f32[64,256]{1,0:T(8,128)S(1)} %get-tuple-element.9.held_corr_ref, bf16[512,256]{1,0:T(8,128)(2,1)S(1)} %get-tuple-element.10.v_hi, bf16[512,256]{1,0:T(8,128)(2,1)S(1)} %get-tuple-element.11.v_lo, ...), custom_call_target="tpu_custom_call" | custom-call | tf_op jit(solution)/shard_map/pallas_call | solution.py:402

commit v6 on v5

--- a/solution.py
+++ b/solution.py
@@ -67,28 +67,26 @@
             src_ref=src, dst_ref=dst, send_sem=send, recv_sem=recv,
             device_id=(row, col), device_id_type=pl.DeviceIdType.MESH)
 
-    sends = []
-
-    def drain():
-        for desc, when in sends:
-            if when is None:
-                desc.wait_send()
-            else:
-                pl.when(when)(desc.wait_send)
-        sends.clear()
-
     def go(desc, when=None):
         if when is None:
             desc.start()
         else:
             pl.when(when)(desc.start)
-        sends.append((desc, when))
+
+    def sent(ref, sem):
+        copy(ref, ref, sem, kg_recv.at[0], r, c).wait_send()
+
+    def landed(ref, sem):
+        copy(ref, ref, kg_send.at[0], sem, r, c).wait_recv()
+
+    def some(ref, h, count):
+        return ref.at[h, pl.ds(0, count * blk), :]
 
     loads = [pltpu.make_async_copy(panel_hbm.at[:, pl.ds(h * hw, hw)], vr.at[h, rows(c, blk), :], local_sem.at[h])
              for h in range(nh)]
     loads.append(pltpu.make_async_copy(a_hbm, a_ref, local_sem.at[nh]))
     loads.append(pltpu.make_async_copy(t_hbm, t_ref, local_sem.at[nh + 1]))
-    for load in loads:
+    for load in loads[:nh]:
         load.start()
 
     across = z * 2 + 1 - y
@@ -98,11 +96,13 @@
     def greet(row, col):
         pl.semaphore_signal(barrier, inc=1, device_id=(row, col), device_id_type=pl.DeviceIdType.MESH)
 
-    for d in range(1, lines):
+    for d in reversed(range(1, lines)):
         greet(r, peer(d) * 2 + y)
     greet(r, across)
     for d in range(1, nrows):
         greet(lax.rem(r + d, nrows), c)
+    for load in loads[nh:]:
+        load.start()
     for h in range(nh):
         loads[h].wait()
     pl.semaphore_wait(barrier, lines + nrows - 1)
@@ -110,9 +110,9 @@
     order = list(range(1, lines))
     for h in range(nh):
         own = vr.at[h, rows(c, blk), :]
-        go(copy(own, own, v_send.at[h, z], v_recv.at[h, z], r, across))
+        go(copy(own, own, v_send.at[h], v_recv.at[h, z], r, across))
         for d in order:
-            go(copy(own, own, v_send.at[h, peer(d)], v_recv.at[h, z], r, peer(d) * 2 + y))
+            go(copy(own, own, v_send.at[h], v_recv.at[h, z], r, peer(d) * 2 + y))
 
     loads[nh].wait()
 
@@ -125,16 +125,12 @@
     t_two = split(t_ref[...])
     tt_two = split(t_ref[...].T)
 
-    def arrived(h, line, side, recv):
-        slot = vr.at[h, rows(line * 2 + side, blk), :]
-        copy(slot, slot, v_send.at[h, line], recv.at[h, line], r, c).wait_recv()
-        return slot
-
     for h in range(nh):
         for d in range(1, lines):
             line = peer(d)
-            slot = arrived(h, line, y, v_recv)
-            go(copy(slot, slot, vf_send.at[h, line], vf_recv.at[h, line], r, across))
+            slot = vr.at[h, rows(line * 2 + y, blk), :]
+            landed(slot, v_recv.at[h, line])
+            go(copy(slot, slot, vf_send.at[h], vf_recv.at[h, d // 2], r, across))
 
     holder = c * nrows // ncols
     first_block = lax.rem(c * nrows, ncols)
@@ -144,8 +140,8 @@
         held = vr.at[h, rows(first_block // nrows, wide), :]
         kept = vc.at[h]
         for d in range(1, nrows // 2):
-            go(copy(held, kept, vc_send.at[h, d], vc_recv.at[h], lax.rem(r + 2 * d, nrows), c), r == holder)
-        go(copy(held, kept, vc_send.at[h, 0], vc_recv.at[h], mate, c), r == holder)
+            go(copy(held, kept, vc_send.at[h], vc_recv.at[h], lax.rem(r + 2 * d, nrows), c), r == holder)
+        go(copy(held, kept, vc_send.at[h], vc_recv.at[h], mate, c), r == holder)
 
         @pl.when(r == holder)
         def _():
@@ -156,19 +152,20 @@
 
         @pl.when(r != holder)
         def _():
-            copy(kept, kept, vc_send.at[h, 0], vc_recv.at[h], r, c).wait_recv()
-        go(copy(kept, kept, vc_send.at[h, 0], vc_recv.at[h], mate, c), (r != holder) & same)
+            landed(kept, vc_recv.at[h])
+        go(copy(kept, kept, vc_send.at[h], vc_recv.at[h], mate, c), (r != holder) & same)
 
     def reduce_product(h):
         for e in range(tiles):
-            for d in (2 * e, 2 * e + 1):
-                arrived(h, peer(d), 1 - y, vf_recv if d else v_recv)
+            if e == 0:
+                landed(some(vr, h, 1), v_recv.at[h, z])
+            landed(some(vr, h, 2 if e else 1), vf_recv.at[h, e])
             i = peer(2 * e) // 2
             part = mult((at_hi[i], at_lo[i]), split(vr[h, rows(i, tile), :]))
             q[h] = part if e == 0 else q[h] + part
         for d in range(1, nrows):
             other = lax.rem(r + d, nrows)
-            go(copy(q.at[h, rows(other, blk), :], qin.at[h, d], q_send.at[h, d], q_recv.at[h, d], other, c))
+            go(copy(q.at[h, rows(other, blk), :], qin.at[h, d], q_send.at[h], q_recv.at[h], other, c))
 
     reduce_product(0)
     hand_panel(0)
@@ -187,8 +184,7 @@
     here = r * group + lax.rem(z, group)
     products = []
     for h in range(nh):
-        for d in range(1, nrows):
-            copy(qin.at[h, d], qin.at[h, d], q_send.at[h, d], q_recv.at[h, d], r, c).wait_recv()
+        landed(qin.at[h, pl.ds(1, nrows - 1)], q_recv.at[h])
         product = q[h, rows(r, blk), :]
         for d in range(1, nrows):
             product = product + qin[h, d]
@@ -202,21 +198,19 @@
         mine[...] = scaled
         slot = sr.at[h, rows(place, blk), :]
         for d in order:
-            go(copy(mine, slot, s_send.at[h, peer(d)], s_recv.at[h, here], target, peer(d) * 2 + y))
+            go(copy(mine, slot, s_send.at[h], s_recv.at[h, here], target, peer(d) * 2 + y))
         for d in range(1, nrows // 2):
-            go(copy(mine, mine, sc_send.at[h, 2 * d], sc_recv.at[h, 2 * d], lax.rem(r + 2 * d, nrows), c))
-        go(copy(mine, mine, sc_send.at[h, 1], sc_recv.at[h, 1], mate, c))
+            go(copy(mine, mine, sc_send.at[h], sc_recv.at[h, d], lax.rem(r + 2 * d, nrows), c))
+        go(copy(mine, mine, sc_send.at[h], sc_recv.at[h, 0], mate, c))
 
     def from_mate(h):
-        for d in range(nrows // 2):
-            slot = sc.at[h, rows(lax.rem(mate - 2 * d + nrows, nrows), blk), :]
-            copy(slot, slot, sc_send.at[h, 2 * d + 1], sc_recv.at[h, 2 * d + 1], r, c).wait_recv()
+        landed(some(sc, h, nrows // 2), sc_recv.at[h, 0])
 
     def forward_scaled(h):
         for d in range(1, nrows // 2):
             slot = sc.at[h, rows(lax.rem(r - 2 * d + nrows, nrows), blk), :]
-            copy(slot, slot, sc_send.at[h, 2 * d], sc_recv.at[h, 2 * d], r, c).wait_recv()
-            go(copy(slot, slot, sc_send.at[h, 2 * d + 1], sc_recv.at[h, 2 * d + 1], mate, c))
+            landed(slot, sc_recv.at[h, d])
+            go(copy(slot, slot, sc_send.at[h], sc_recv.at[h, 0], mate, c))
         pl.when(target == r)(functools.partial(from_mate, h))
         for g in range(group):
             line = r * group + g
@@ -225,9 +219,8 @@
                 at = j * group + g
                 slot = sr.at[h, rows(lax.rem((line * 2 + y) * nrows + j, ncols), blk), :]
                 held = sc.at[h, rows(j, blk), :]
-                straight = copy(held, slot, sf_send.at[h, at], sf_recv.at[h, at], r, across)
-                passed = copy(slot, slot, sf_send.at[h, at], sf_recv.at[h, at], r, across)
-                came = copy(slot, slot, s_send.at[h, 0], s_recv.at[h, at], r, c)
+                straight = copy(held, slot, sf_send.at[h], sf_recv.at[h], r, across)
+                passed = copy(slot, slot, sf_send.at[h], sf_recv.at[h], r, across)
 
                 @pl.when(z == line)
                 def _():
@@ -236,17 +229,11 @@
 
                 @pl.when(z != line)
                 def _():
-                    came.wait_recv()
+                    landed(slot, s_recv.at[h, at])
                     passed.start()
-                sends.append((passed, None))
 
     def gather_scaled(h):
-        for g in range(group):
-            line = r * group + g
-            for j in range(nrows):
-                at = j * group + g
-                slot = sr.at[h, rows(lax.rem((line * 2 + 1 - y) * nrows + j, ncols), blk), :]
-                copy(slot, slot, sf_send.at[h, at], sf_recv.at[h, at], r, c).wait_recv()
+        landed(some(sr, h, nrows * group), sf_recv.at[h])
 
     def small(h, part, base):
         part[...] = jnp.zeros_like(part)
@@ -258,18 +245,17 @@
 
     def pair_up(h, part, room, pair):
         size = pair.shape[0]
-        go(copy(part.at[rows(mate % 2, size), :], room.at[0], k_send.at[h, 0], k_recv.at[h, 0], mate, c))
-        copy(room.at[0], room.at[0], k_send.at[h, 0], k_recv.at[h, 0], r, c).wait_recv()
+        go(copy(part.at[rows(mate % 2, size), :], room.at[0], k_send.at[h], k_recv.at[h, 0], mate, c))
+        landed(room.at[0], k_recv.at[h, 0])
         pair[...] = part[rows(r % 2, size), :] + room[0]
 
-    def spread(h, room, pair, slots):
+    def spread(h, step, room, pair, slots):
         for i in slots:
             row, col = lax.rem(r + i // 2 * 2, nrows), across if i % 2 else c
-            go(copy(pair, room.at[i], k_send.at[h, i], k_recv.at[h, i], row, col))
-
-    def collect(h, room, pair, slots):
-        for i in slots:
-            copy(pair, room.at[i], k_send.at[h, i], k_recv.at[h, i], r, c).wait_recv()
+            go(copy(pair, room.at[i], k_send.at[h], k_recv.at[h, step], row, col))
+
+    def collect(h, step, room, pair, slots):
+        landed(room.at[pl.ds(0, len(slots))], k_recv.at[h, step])
         summed = pair[...]
         for i in slots:
             summed = summed + room[i]
@@ -282,29 +268,27 @@
 
     def completed(h, pair, full):
         other = full.at[rows(mate % 2, pair.shape[0]), :]
-        copy(other, other, kg_send.at[h], kg_recv.at[h], r, c).wait_recv()
+        landed(other, kg_recv.at[h])
         return split(full[...])
 
     hand_panel(1)
-    older = sends[:]
-    sends.clear()
     forward_scaled(0)
     small(0, kpart, 0)
     pair_up(0, kpart, kin, kpair)
-    spread(0, kin, kpair, range(2, nrows, 2))
+    spread(0, 1, kin, kpair, range(2, nrows, 2))
     forward_scaled(1)
     small(1, lpart, hw)
     pair_up(1, lpart, lin, lpair)
-    spread(1, lin, lpair, range(1, nrows))
+    spread(1, 1, lin, lpair, range(1, nrows))
     pass_panel(0)
-
-
-    newer = sends[:]
-    sends[:] = older
-    drain()
-    sends[:] = newer
-    kside[...] = collect(0, kin, kpair, range(2, nrows, 2))
-    spread(0, kin, kside, (1,))
+    for h in range(nh):
+        sent(some(vr, h, lines), v_send.at[h])
+        sent(some(vr, h, lines - 1), vf_send.at[h])
+        sent(some(q, h, nrows - 1), q_send.at[h])
+        sent(some(sr, h, lines - 1), s_send.at[h])
+        sent(some(sc, h, nrows - 1), sc_send.at[h])
+    kside[...] = collect(0, 1, kin, kpair, range(2, nrows, 2))
+    spread(0, 2, kin, kside, (1,))
     gather_scaled(0)
 
     pass_panel(1)
@@ -318,8 +302,8 @@
         out_ref[span, :] = a_ref[span, :] - mult(split(wide_of(sr, span)), vc_two, NT)
     tile_loop(tiles, first)
 
-    finish_half(1, lfull, collect(1, lin, lpair, range(1, nrows)))
-    finish_half(0, kfull, collect(0, kin, kside, (1,)))
+    finish_half(1, lfull, collect(1, 1, lin, lpair, range(1, nrows)))
+    finish_half(0, kfull, collect(0, 2, kin, kside, (1,)))
     for h in range(nh):
         pl.when(target != r)(functools.partial(from_mate, h))
     completed(0, kpair, kfull)
@@ -330,7 +314,19 @@
     y_hi[...], y_lo[...] = split(wide_of(sc, everything) - mult(vc_two, k_two))
     mine = rows(c, blk)
     corr_ref[...] = wide_of(sr, mine) - 0.5 * mult((v_hi[mine, :], v_lo[mine, :]), k_two)
-    drain()
+    for h, room, count in ((0, kin, nrows // 2 + 1), (1, lin, nrows)):
+        sent(some(sr, h, nrows * group), sf_send.at[h])
+        sent(room.at[pl.ds(0, count)], k_send.at[h])
+
+        @pl.when(r == holder)
+        def _():
+            sent(vr.at[h, pl.ds(0, nrows // 2 * wide), :], vc_send.at[h])
+
+        @pl.when((r != holder) & same)
+        def _():
+            sent(vc.at[h], vc_send.at[h])
+    sent(kfull.at[pl.ds(0, kpair.shape[0]), :], kg_send.at[0])
+    sent(lfull.at[pl.ds(0, lpair.shape[0]), :], kg_send.at[1])
 
 
 def hand_out(tile, held_ref, held_corr_ref, v_hi, v_lo, y_hi, y_lo, out_hbm, corr_hbm, stage, sem):
@@ -389,12 +385,11 @@
             pltpu.VMEM((tiles, width, tile), BF16),
             pltpu.VMEM((tiles, width, tile), BF16),
             dma((nh + 2,)),
-            dma((nh, lines)), dma((nh, lines)), dma((nh, lines)), dma((nh, lines)),
-            dma((nh, nrows)), dma((nh, nrows)),
-            dma((nh, lines)), dma((nh, nrows * group)),
-            dma((nh, nrows * group)), dma((nh, nrows * group)),
-            dma((nh, nrows)), dma((nh, nrows)),
-            dma((nh, nrows)), dma((nh,)), dma((nh, nrows)), dma((nh, nrows)), dma((nh,)), dma((nh,)),
+            dma((nh,)), dma((nh, lines)), dma((nh,)), dma((nh, lines // 2)),
+            dma((nh,)), dma((nh,)),
+            dma((nh,)), dma((nh, nrows * group)), dma((nh,)), dma((nh,)),
+            dma((nh,)), dma((nh, nrows // 2)),
+            dma((nh,)), dma((nh,)), dma((nh,)), dma((nh, 3)), dma((nh,)), dma((nh,)),
         ],
         compiler_params=pltpu.CompilerParams(
             collective_id=0, has_side_effects=True, vmem_limit_bytes=limit),

time: 35.4 us -> 34.7 us (0.980)
  Pallas kernels: 34.6 us -> 33.9 us
    pallas_call x1, Pallas kernels: 33.4 us -> 32.7 us  [per_device(): pl.pallas_call(functools.partial(kernel, nrows, ncols, tile), out_shape=(...]
where the time goes in v6:
time: 34.7 us; the launch traced here: 34.5 us
  Pallas kernels  33.9 us (98%)
  between operations  0.64 us (2%)
    pallas_call x1, Pallas kernels, per_device(): pl.pallas_call(functools.partial(kernel, nrows, ncols, tile), out_shape=(...  32.7 us
    pallas_call x1, Pallas kernels, per_device(): pl.pallas_call(functools.partial(hand_out, tile), out_shape=(jax.ShapeDty...  1.22 us

profile of v6, /device:TPU:1, one launch (start us, length us, event | category | flops | bytes accessed | tf_op | source)
XLA Modules:
  0.0 34.5 jit_solution(13942927329635381926)
XLA Ops:
  0.6 32.7 %shard_map.50 = (f32[512,256]{1,0:T(8,128)S(1)}, f32[64,256]{1,0:T(8,128)S(1)}, bf16[512,256]{1,0:T(8,128)(2,1)S(1)}, bf16[512,256]{1,0:T(8,128)(2,1)S(1)}, bf16...) custom-call(f32[512,256]{1,0:T(8,128)} %a_hbm.1, f32[64,256]{1,0:T(8,128)} %panel_hbm.1, f32[256,256]{1,0:T(8,128)} %t_hbm.1), custom_call_target="tpu_custom_call" | custom-call | tf_op jit(solution)/shard_map/pallas_call | solution.py:358
  33.3 1.2 %shard_map.51 = (f32[512,256]{1,0:T(8,128)}, f32[64,256]{1,0:T(8,128)}) custom-call(f32[512,256]{1,0:T(8,128)S(1)} %get-tuple-element.8.held_ref, f32[64,256]{1,0:T(8,128)S(1)} %get-tuple-element.9.held_corr_ref, bf16[512,256]{1,0:T(8,128)(2,1)S(1)} %get-tuple-element.10.v_hi, bf16[512,256]{1,0:T(8,128)(2,1)S(1)} %get-tuple-element.11.v_lo, ...), custom_call_target="tpu_custom_call" | custom-call | tf_op jit(solution)/shard_map/pallas_call | solution.py:397

commit v7 on v6

--- a/solution.py
+++ b/solution.py
@@ -39,9 +39,8 @@
            a_ref, t_ref, vr, vc, sr, sc, q, qin, kpart, kin, kpair, kside, kfull,
            lpart, lin, lpair, lfull,
            at_hi, at_lo, vt_hi, vt_lo,
-           local_sem, v_send, v_recv, vf_send, vf_recv, q_send, q_recv,
-           s_send, s_recv, sf_send, sf_recv, sc_send, sc_recv,
-           vc_send, vc_recv, k_send, k_recv, kg_send, kg_recv):
+           local_sem, v_send, v_recv, vf_recv, q_send, q_recv, s_recv, sf_recv, sc_send, sc_recv,
+           vc_send, vc_recv, k_send, k_recv, kg_recv):
     r, c = lax.axis_index("row"), lax.axis_index("col")
     lines = ncols // 2
     group = ncols // (2 * nrows)
@@ -77,7 +76,7 @@
         copy(ref, ref, sem, kg_recv.at[0], r, c).wait_send()
 
     def landed(ref, sem):
-        copy(ref, ref, kg_send.at[0], sem, r, c).wait_recv()
+        copy(ref, ref, k_send.at[0], sem, r, c).wait_recv()
 
     def some(ref, h, count):
         return ref.at[h, pl.ds(0, count * blk), :]
@@ -110,9 +109,9 @@
     order = list(range(1, lines))
     for h in range(nh):
         own = vr.at[h, rows(c, blk), :]
-        go(copy(own, own, v_send.at[h], v_recv.at[h, z], r, across))
+        go(copy(own, own, v_send.at[0], v_recv.at[h, z], r, across))
         for d in order:
-            go(copy(own, own, v_send.at[h], v_recv.at[h, z], r, peer(d) * 2 + y))
+            go(copy(own, own, v_send.at[0], v_recv.at[h, z], r, peer(d) * 2 + y))
 
     loads[nh].wait()
 
@@ -130,7 +129,7 @@
             line = peer(d)
             slot = vr.at[h, rows(line * 2 + y, blk), :]
             landed(slot, v_recv.at[h, line])
-            go(copy(slot, slot, vf_send.at[h], vf_recv.at[h, d // 2], r, across))
+            go(copy(slot, slot, v_send.at[0], vf_recv.at[h, d // 2], r, across))
 
     holder = c * nrows // ncols
     first_block = lax.rem(c * nrows, ncols)
@@ -140,8 +139,8 @@
         held = vr.at[h, rows(first_block // nrows, wide), :]
         kept = vc.at[h]
         for d in range(1, nrows // 2):
-            go(copy(held, kept, vc_send.at[h], vc_recv.at[h], lax.rem(r + 2 * d, nrows), c), r == holder)
-        go(copy(held, kept, vc_send.at[h], vc_recv.at[h], mate, c), r == holder)
+            go(copy(held, kept, vc_send.at[0], vc_recv.at[h], lax.rem(r + 2 * d, nrows), c), r == holder)
+        go(copy(held, kept, vc_send.at[0], vc_recv.at[h], mate, c), r == holder)
 
         @pl.when(r == holder)
         def _():
@@ -153,7 +152,7 @@
         @pl.when(r != holder)
         def _():
             landed(kept, vc_recv.at[h])
-        go(copy(kept, kept, vc_send.at[h], vc_recv.at[h], mate, c), (r != holder) & same)
+        go(copy(kept, kept, vc_send.at[0], vc_recv.at[h], mate, c), (r != holder) & same)
 
     def reduce_product(h):
         for e in range(tiles):
@@ -165,7 +164,7 @@
             q[h] = part if e == 0 else q[h] + part
         for d in range(1, nrows):
             other = lax.rem(r + d, nrows)
-            go(copy(q.at[h, rows(other, blk), :], qin.at[h, d], q_send.at[h], q_recv.at[h], other, c))
+            go(copy(q.at[h, rows(other, blk), :], qin.at[h, d], q_send.at[0], q_recv.at[h], other, c))
 
     reduce_product(0)
     hand_panel(0)
@@ -197,11 +196,11 @@
         mine = sc.at[h, rows(r, blk), :]
         mine[...] = scaled
         slot = sr.at[h, rows(place, blk), :]
-        for d in order:
-            go(copy(mine, slot, s_send.at[h], s_recv.at[h, here], target, peer(d) * 2 + y))
+        for d in [1] + order[:0:-1]:
+            go(copy(mine, slot, q_send.at[0], s_recv.at[h, here], target, peer(d) * 2 + y))
         for d in range(1, nrows // 2):
-            go(copy(mine, mine, sc_send.at[h], sc_recv.at[h, d], lax.rem(r + 2 * d, nrows), c))
-        go(copy(mine, mine, sc_send.at[h], sc_recv.at[h, 0], mate, c))
+            go(copy(mine, mine, sc_send.at[0], sc_recv.at[h, d], lax.rem(r + 2 * d, nrows), c))
+        go(copy(mine, mine, sc_send.at[0], sc_recv.at[h, 0], mate, c))
 
     def from_mate(h):
         landed(some(sc, h, nrows // 2), sc_recv.at[h, 0])
@@ -210,7 +209,7 @@
         for d in range(1, nrows // 2):
             slot = sc.at[h, rows(lax.rem(r - 2 * d + nrows, nrows), blk), :]
             landed(slot, sc_recv.at[h, d])
-            go(copy(slot, slot, sc_send.at[h], sc_recv.at[h, 0], mate, c))
+            go(copy(slot, slot, sc_send.at[0], sc_recv.at[h, 0], mate, c))
         pl.when(target == r)(functools.partial(from_mate, h))
         for g in range(group):
             line = r * group + g
@@ -219,8 +218,8 @@
                 at = j * group + g
                 slot = sr.at[h, rows(lax.rem((line * 2 + y) * nrows + j, ncols), blk), :]
                 held = sc.at[h, rows(j, blk), :]
-                straight = copy(held, slot, sf_send.at[h], sf_recv.at[h], r, across)
-                passed = copy(slot, slot, sf_send.at[h], sf_recv.at[h], r, across)
+                straight = copy(held, slot, sc_send.at[0], sf_recv.at[h], r, across)
+                passed = copy(slot, slot, sc_send.at[0], sf_recv.at[h], r, across)
 
                 @pl.when(z == line)
                 def _():
@@ -245,14 +244,14 @@
 
     def pair_up(h, part, room, pair):
         size = pair.shape[0]
-        go(copy(part.at[rows(mate % 2, size), :], room.at[0], k_send.at[h], k_recv.at[h, 0], mate, c))
+        go(copy(part.at[rows(mate % 2, size), :], room.at[0], k_send.at[0], k_recv.at[h, 0], mate, c))
         landed(room.at[0], k_recv.at[h, 0])
         pair[...] = part[rows(r % 2, size), :] + room[0]
 
     def spread(h, step, room, pair, slots):
         for i in slots:
             row, col = lax.rem(r + i // 2 * 2, nrows), across if i % 2 else c
-            go(copy(pair, room.at[i], k_send.at[h], k_recv.at[h, step], row, col))
+            go(copy(pair, room.at[i], k_send.at[0], k_recv.at[h, step], row, col))
 
     def collect(h, step, room, pair, slots):
         landed(room.at[pl.ds(0, len(slots))], k_recv.at[h, step])
@@ -264,12 +263,8 @@
     def finish_half(h, full, summed):
         mine = full.at[rows(r % 2, summed.shape[0]), :]
         mine[...] = summed
-        go(copy(mine, mine, kg_send.at[h], kg_recv.at[h], mate, c))
-
-    def completed(h, pair, full):
-        other = full.at[rows(mate % 2, pair.shape[0]), :]
-        landed(other, kg_recv.at[h])
-        return split(full[...])
+        go(copy(mine, mine, k_send.at[0], kg_recv.at[0], mate, c))
+
 
     hand_panel(1)
     forward_scaled(0)
@@ -281,12 +276,8 @@
     pair_up(1, lpart, lin, lpair)
     spread(1, 1, lin, lpair, range(1, nrows))
     pass_panel(0)
-    for h in range(nh):
-        sent(some(vr, h, lines), v_send.at[h])
-        sent(some(vr, h, lines - 1), vf_send.at[h])
-        sent(some(q, h, nrows - 1), q_send.at[h])
-        sent(some(sr, h, lines - 1), s_send.at[h])
-        sent(some(sc, h, nrows - 1), sc_send.at[h])
+    sent(vr.at[:, pl.ds(0, (2 * lines - 1) * blk), :], v_send.at[0])
+    sent(sr.at[:, pl.ds(0, (nrows + lines - 2) * blk), :], q_send.at[0])
     kside[...] = collect(0, 1, kin, kpair, range(2, nrows, 2))
     spread(0, 2, kin, kside, (1,))
     gather_scaled(0)
@@ -306,27 +297,24 @@
     finish_half(0, kfull, collect(0, 2, kin, kside, (1,)))
     for h in range(nh):
         pl.when(target != r)(functools.partial(from_mate, h))
-    completed(0, kpair, kfull)
-    completed(1, lpair, lfull)
+    landed(vr.at[0, pl.ds(0, kpair.shape[0] + lpair.shape[0]), :], kg_recv.at[0])
     left = kfull[...]
     right = jnp.concatenate([left[hw:, :].T, lfull[...]], axis=0)
     k_two = split(jnp.concatenate([left, right], axis=1))
     y_hi[...], y_lo[...] = split(wide_of(sc, everything) - mult(vc_two, k_two))
     mine = rows(c, blk)
     corr_ref[...] = wide_of(sr, mine) - 0.5 * mult((v_hi[mine, :], v_lo[mine, :]), k_two)
-    for h, room, count in ((0, kin, nrows // 2 + 1), (1, lin, nrows)):
-        sent(some(sr, h, nrows * group), sf_send.at[h])
-        sent(room.at[pl.ds(0, count)], k_send.at[h])
-
-        @pl.when(r == holder)
-        def _():
-            sent(vr.at[h, pl.ds(0, nrows // 2 * wide), :], vc_send.at[h])
-
-        @pl.when((r != holder) & same)
-        def _():
-            sent(vc.at[h], vc_send.at[h])
-    sent(kfull.at[pl.ds(0, kpair.shape[0]), :], kg_send.at[0])
-    sent(lfull.at[pl.ds(0, lpair.shape[0]), :], kg_send.at[1])
+    sent(sr.at[:, pl.ds(0, (nrows - 1 + nrows * group) * blk), :], sc_send.at[0])
+
+    @pl.when(r == holder)
+    def _():
+        sent(vr.at[:, pl.ds(0, nrows // 2 * wide), :], vc_send.at[0])
+
+    @pl.when((r != holder) & same)
+    def _():
+        sent(vc, vc_send.at[0])
+    moved = (nrows // 2 + 2) * kpair.shape[0] + (nrows + 1) * lpair.shape[0]
+    sent(vr.at[:, pl.ds(0, moved // nh), :], k_send.at[0])
 
 
 def hand_out(tile, held_ref, held_corr_ref, v_hi, v_lo, y_hi, y_lo, out_hbm, corr_hbm, stage, sem):
@@ -385,11 +373,10 @@
             pltpu.VMEM((tiles, width, tile), BF16),
             pltpu.VMEM((tiles, width, tile), BF16),
             dma((nh + 2,)),
-            dma((nh,)), dma((nh, lines)), dma((nh,)), dma((nh, lines // 2)),
-            dma((nh,)), dma((nh,)),
-            dma((nh,)), dma((nh, nrows * group)), dma((nh,)), dma((nh,)),
-            dma((nh,)), dma((nh, nrows // 2)),
-            dma((nh,)), dma((nh,)), dma((nh,)), dma((nh, 3)), dma((nh,)), dma((nh,)),
+            dma((1,)), dma((nh, lines)), dma((nh, lines // 2)),
+            dma((1,)), dma((nh,)), dma((nh, nrows * group)), dma((nh,)),
+            dma((1,)), dma((nh, nrows // 2)),
+            dma((1,)), dma((nh,)), dma((1,)), dma((nh, 3)), dma((1,)),
         ],
         compiler_params=pltpu.CompilerParams(
             collective_id=0, has_side_effects=True, vmem_limit_bytes=limit),

time: 34.7 us -> 34.3 us (0.988)
  Pallas kernels: 33.9 us -> 33.3 us
    pallas_call x1, Pallas kernels: 32.7 us -> 32.1 us  [per_device(): pl.pallas_call(functools.partial(kernel, nrows, ncols, tile), out_shape=(...]
where the time goes in v7:
time: 34.3 us; the launch traced here: 34 us
  Pallas kernels  33.3 us (97%)
  between operations  0.64 us (2%)
    pallas_call x1, Pallas kernels, per_device(): pl.pallas_call(functools.partial(kernel, nrows, ncols, tile), out_shape=(...  32.1 us
    pallas_call x1, Pallas kernels, per_device(): pl.pallas_call(functools.partial(hand_out, tile), out_shape=(jax.ShapeDty...  1.22 us

profile of v7, /device:TPU:1, one launch (start us, length us, event | category | flops | bytes accessed | tf_op | source)
XLA Modules:
  0.0 34.0 jit_solution(5926853366020238016)
XLA Ops:
  0.6 32.1 %shard_map.50 = (f32[512,256]{1,0:T(8,128)S(1)}, f32[64,256]{1,0:T(8,128)S(1)}, bf16[512,256]{1,0:T(8,128)(2,1)S(1)}, bf16[512,256]{1,0:T(8,128)(2,1)S(1)}, bf16...) custom-call(f32[512,256]{1,0:T(8,128)} %a_hbm.1, f32[64,256]{1,0:T(8,128)} %panel_hbm.1, f32[256,256]{1,0:T(8,128)} %t_hbm.1), custom_call_target="tpu_custom_call" | custom-call | tf_op jit(solution)/shard_map/pallas_call | solution.py:346
  32.7 1.2 %shard_map.51 = (f32[512,256]{1,0:T(8,128)}, f32[64,256]{1,0:T(8,128)}) custom-call(f32[512,256]{1,0:T(8,128)S(1)} %get-tuple-element.8.held_ref, f32[64,256]{1,0:T(8,128)S(1)} %get-tuple-element.9.held_corr_ref, bf16[512,256]{1,0:T(8,128)(2,1)S(1)} %get-tuple-element.10.v_hi, bf16[512,256]{1,0:T(8,128)(2,1)S(1)} %get-tuple-element.11.v_lo, ...), custom_call_target="tpu_custom_call" | custom-call | tf_op jit(solution)/shard_map/pallas_call | solution.py:384

commit v8 on v7

--- a/solution.py
+++ b/solution.py
@@ -177,7 +177,6 @@
         high, low = split(mult(tt_two, v_two, NT))
         vt_hi[i] = high
         vt_lo[i] = low
-    tile_loop(tiles, turn)
 
     place = lax.rem(c * nrows + r, ncols)
     here = r * group + lax.rem(z, group)
@@ -201,20 +200,26 @@
         for d in range(1, nrows // 2):
             go(copy(mine, mine, sc_send.at[0], sc_recv.at[h, d], lax.rem(r + 2 * d, nrows), c))
         go(copy(mine, mine, sc_send.at[0], sc_recv.at[h, 0], mate, c))
+        if h == 0:
+            hand_panel(1)
+            tile_loop(tiles, turn)
 
     def from_mate(h):
         landed(some(sc, h, nrows // 2), sc_recv.at[h, 0])
 
-    def forward_scaled(h):
+    def hand_on(h):
         for d in range(1, nrows // 2):
             slot = sc.at[h, rows(lax.rem(r - 2 * d + nrows, nrows), blk), :]
             landed(slot, sc_recv.at[h, d])
             go(copy(slot, slot, sc_send.at[0], sc_recv.at[h, 0], mate, c))
+
+    def forward_scaled(h):
+        pl.when(target // 2 == r // 2)(functools.partial(hand_on, h))
         pl.when(target == r)(functools.partial(from_mate, h))
         for g in range(group):
             line = r * group + g
             for d in range(nrows):
-                j = lax.rem(r + d, nrows)
+                j = lax.rem((mate if d % 2 else r) + d // 2 * 2, nrows)
                 at = j * group + g
                 slot = sr.at[h, rows(lax.rem((line * 2 + y) * nrows + j, ncols), blk), :]
                 held = sc.at[h, rows(j, blk), :]
@@ -230,6 +235,7 @@
                 def _():
                     landed(slot, s_recv.at[h, at])
                     passed.start()
+
 
     def gather_scaled(h):
         landed(some(sr, h, nrows * group), sf_recv.at[h])
@@ -266,7 +272,6 @@
         go(copy(mine, mine, k_send.at[0], kg_recv.at[0], mate, c))
 
 
-    hand_panel(1)
     forward_scaled(0)
     small(0, kpart, 0)
     pair_up(0, kpart, kin, kpair)
@@ -275,33 +280,39 @@
     small(1, lpart, hw)
     pair_up(1, lpart, lin, lpair)
     spread(1, 1, lin, lpair, range(1, nrows))
+    for h in range(nh):
+        pl.when(target // 2 != r // 2)(functools.partial(hand_on, h))
     pass_panel(0)
     sent(vr.at[:, pl.ds(0, (2 * lines - 1) * blk), :], v_send.at[0])
     sent(sr.at[:, pl.ds(0, (nrows + lines - 2) * blk), :], q_send.at[0])
     kside[...] = collect(0, 1, kin, kpair, range(2, nrows, 2))
     spread(0, 2, kin, kside, (1,))
     gather_scaled(0)
-
     pass_panel(1)
-    gather_scaled(1)
-
+    for h in range(nh):
+        pl.when(target != r)(functools.partial(from_mate, h))
     everything = pl.ds(0, wide)
-    vc_two = split(wide_of(vc, everything))
+    sc_turned = wide_of(sc, everything).T
+    vc_turned = split(wide_of(vc, everything).T)
+    vc_near, vc_rest = (tuple(v[h * hw:(h + 1) * hw, :] for v in vc_turned) for h in range(nh))
 
     def first(i):
         span = pl.ds(pl.multiple_of(i * tile, tile), tile)
-        out_ref[span, :] = a_ref[span, :] - mult(split(wide_of(sr, span)), vc_two, NT)
+        out_ref[span, :] = a_ref[span, :] - mult(split(sr[0, span, :]), vc_near)
     tile_loop(tiles, first)
 
+    def second(i):
+        span = pl.ds(pl.multiple_of(i * tile, tile), tile)
+        out_ref[span, :] = out_ref[span, :] - mult(split(sr[1, span, :]), vc_rest)
     finish_half(1, lfull, collect(1, 1, lin, lpair, range(1, nrows)))
     finish_half(0, kfull, collect(0, 2, kin, kside, (1,)))
-    for h in range(nh):
-        pl.when(target != r)(functools.partial(from_mate, h))
+    gather_scaled(1)
+    tile_loop(tiles, second)
     landed(vr.at[0, pl.ds(0, kpair.shape[0] + lpair.shape[0]), :], kg_recv.at[0])
     left = kfull[...]
     right = jnp.concatenate([left[hw:, :].T, lfull[...]], axis=0)
     k_two = split(jnp.concatenate([left, right], axis=1))
-    y_hi[...], y_lo[...] = split(wide_of(sc, everything) - mult(vc_two, k_two))
+    y_hi[...], y_lo[...] = split(sc_turned - mult(k_two, vc_turned))
     mine = rows(c, blk)
     corr_ref[...] = wide_of(sr, mine) - 0.5 * mult((v_hi[mine, :], v_lo[mine, :]), k_two)
     sent(sr.at[:, pl.ds(0, (nrows - 1 + nrows * group) * blk), :], sc_send.at[0])
@@ -323,7 +334,7 @@
     copies[0].start()
     for i in range(tiles):
         span = pl.ds(i * tile, tile)
-        stage[span, :] = held_ref[span, :] - mult((v_hi[span, :], v_lo[span, :]), (y_hi[...], y_lo[...]), NT)
+        stage[span, :] = held_ref[span, :] - mult((v_hi[span, :], v_lo[span, :]), (y_hi[...], y_lo[...]))
         copies.append(pltpu.make_async_copy(stage.at[span, :], out_hbm.at[span, :], sem.at[i]))
         copies[-1].start()
     for copy in copies:
@@ -347,7 +358,7 @@
         functools.partial(kernel, nrows, ncols, tile),
         out_shape=(jax.ShapeDtypeStruct(matrix.shape, F32), jax.ShapeDtypeStruct(panel.shape, F32),
                    jax.ShapeDtypeStruct((total, width), BF16), jax.ShapeDtypeStruct((total, width), BF16),
-                   jax.ShapeDtypeStruct((wide, width), BF16), jax.ShapeDtypeStruct((wide, width), BF16)),
+                   jax.ShapeDtypeStruct((width, wide), BF16), jax.ShapeDtypeStruct((width, wide), BF16)),
         in_specs=[hbm] * 3,
         out_specs=(vmem,) * 6,
         scratch_shapes=[

time: 34.3 us -> 34.3 us (level)
  no operation moved by 1% of the time
where the time goes in v8:
time: 34.3 us; the launch traced here: 33.9 us
  Pallas kernels  33.3 us (97%)
  between operations  0.64 us (2%)
    pallas_call x1, Pallas kernels, per_device(): pl.pallas_call(functools.partial(kernel, nrows, ncols, tile), out_shape=(...  32.1 us
    pallas_call x1, Pallas kernels, per_device(): pl.pallas_call(functools.partial(hand_out, tile), out_shape=(jax.ShapeDty...  1.19 us

profile of v8, /device:TPU:1, one launch (start us, length us, event | category | flops | bytes accessed | tf_op | source)
XLA Modules:
  0.0 33.9 jit_solution(7761456828349948019)
XLA Ops:
  0.6 32.1 %shard_map.50 = (f32[512,256]{1,0:T(8,128)S(1)}, f32[64,256]{1,0:T(8,128)S(1)}, bf16[512,256]{1,0:T(8,128)(2,1)S(1)}, bf16[512,256]{1,0:T(8,128)(2,1)S(1)}, bf16...) custom-call(f32[512,256]{1,0:T(8,128)} %a_hbm.1, f32[64,256]{1,0:T(8,128)} %panel_hbm.1, f32[256,256]{1,0:T(8,128)} %t_hbm.1), custom_call_target="tpu_custom_call" | custom-call | tf_op jit(solution)/shard_map/pallas_call | solution.py:357
  32.7 1.2 %shard_map.51 = (f32[512,256]{1,0:T(8,128)}, f32[64,256]{1,0:T(8,128)}) custom-call(f32[512,256]{1,0:T(8,128)S(1)} %get-tuple-element.8.held_ref, f32[64,256]{1,0:T(8,128)S(1)} %get-tuple-element.9.held_corr_ref, bf16[512,256]{1,0:T(8,128)(2,1)S(1)} %get-tuple-element.10.v_hi, bf16[512,256]{1,0:T(8,128)(2,1)S(1)} %get-tuple-element.11.v_lo, ...), custom_call_target="tpu_custom_call" | custom-call | tf_op jit(solution)/shard_map/pallas_call | solution.py:395

commit v9 on v8

--- a/solution.py
+++ b/solution.py
@@ -149,10 +149,13 @@
     def pass_panel(h):
         kept = vc.at[h]
 
-        @pl.when(r != holder)
+        @pl.when((r != holder) & same)
         def _():
             landed(kept, vc_recv.at[h])
-        go(copy(kept, kept, vc_send.at[0], vc_recv.at[h], mate, c), (r != holder) & same)
+            copy(kept, kept, vc_send.at[0], vc_recv.at[h], mate, c).start()
+
+    def take_panel(h):
+        pl.when(jnp.logical_not(same))(functools.partial(landed, vc.at[h], vc_recv.at[h]))
 
     def reduce_product(h):
         for e in range(tiles):
@@ -283,12 +286,14 @@
     for h in range(nh):
         pl.when(target // 2 != r // 2)(functools.partial(hand_on, h))
     pass_panel(0)
+    pass_panel(1)
     sent(vr.at[:, pl.ds(0, (2 * lines - 1) * blk), :], v_send.at[0])
     sent(sr.at[:, pl.ds(0, (nrows + lines - 2) * blk), :], q_send.at[0])
     kside[...] = collect(0, 1, kin, kpair, range(2, nrows, 2))
     spread(0, 2, kin, kside, (1,))
     gather_scaled(0)
-    pass_panel(1)
+    take_panel(0)
+    take_panel(1)
     for h in range(nh):
         pl.when(target != r)(functools.partial(from_mate, h))
     everything = pl.ds(0, wide)

time: 34.3 us -> 34.3 us (level)
  no operation moved by 1% of the time
where the time goes in v9:
time: 34.3 us; the launch traced here: 33.9 us
  Pallas kernels  33.3 us (97%)
  between operations  0.64 us (2%)
    pallas_call x1, Pallas kernels, per_device(): pl.pallas_call(functools.partial(kernel, nrows, ncols, tile), out_shape=(...  32.1 us
    pallas_call x1, Pallas kernels, per_device(): pl.pallas_call(functools.partial(hand_out, tile), out_shape=(jax.ShapeDty...  1.19 us

profile of v9, /device:TPU:1, one launch (start us, length us, event | category | flops | bytes accessed | tf_op | source)
XLA Modules:
  0.0 33.9 jit_solution(14665210968316516723)
XLA Ops:
  0.6 32.1 %shard_map.50 = (f32[512,256]{1,0:T(8,128)S(1)}, f32[64,256]{1,0:T(8,128)S(1)}, bf16[512,256]{1,0:T(8,128)(2,1)S(1)}, bf16[512,256]{1,0:T(8,128)(2,1)S(1)}, bf16...) custom-call(f32[512,256]{1,0:T(8,128)} %a_hbm.1, f32[64,256]{1,0:T(8,128)} %panel_hbm.1, f32[256,256]{1,0:T(8,128)} %t_hbm.1), custom_call_target="tpu_custom_call" | custom-call | tf_op jit(solution)/shard_map/pallas_call | solution.py:362
  32.7 1.2 %shard_map.51 = (f32[512,256]{1,0:T(8,128)}, f32[64,256]{1,0:T(8,128)}) custom-call(f32[512,256]{1,0:T(8,128)S(1)} %get-tuple-element.8.held_ref, f32[64,256]{1,0:T(8,128)S(1)} %get-tuple-element.9.held_corr_ref, bf16[512,256]{1,0:T(8,128)(2,1)S(1)} %get-tuple-element.10.v_hi, bf16[512,256]{1,0:T(8,128)(2,1)S(1)} %get-tuple-element.11.v_lo, ...), custom_call_target="tpu_custom_call" | custom-call | tf_op jit(solution)/shard_map/pallas_call | solution.py:400

commit v10 on v9

--- a/solution.py
+++ b/solution.py
@@ -81,10 +81,10 @@
     def some(ref, h, count):
         return ref.at[h, pl.ds(0, count * blk), :]
 
-    loads = [pltpu.make_async_copy(panel_hbm.at[:, pl.ds(h * hw, hw)], vr.at[h, rows(c, blk), :], local_sem.at[h])
+    loads = [pltpu.make_async_copy(panel_hbm.at[:, pl.ds(h * hw, hw)], vr.at[h, rows(c, blk), :], local_sem.at[0])
              for h in range(nh)]
-    loads.append(pltpu.make_async_copy(a_hbm, a_ref, local_sem.at[nh]))
-    loads.append(pltpu.make_async_copy(t_hbm, t_ref, local_sem.at[nh + 1]))
+    loads.append(pltpu.make_async_copy(a_hbm, a_ref, local_sem.at[1]))
+    loads.append(pltpu.make_async_copy(t_hbm, t_ref, local_sem.at[2]))
     for load in loads[:nh]:
         load.start()
 
@@ -102,8 +102,8 @@
         greet(lax.rem(r + d, nrows), c)
     for load in loads[nh:]:
         load.start()
-    for h in range(nh):
-        loads[h].wait()
+    both = vr.at[:, rows(c, blk), :]
+    pltpu.make_async_copy(both, both, local_sem.at[0]).wait()
     pl.semaphore_wait(barrier, lines + nrows - 1)
 
     order = list(range(1, lines))
@@ -253,17 +253,17 @@
 
     def pair_up(h, part, room, pair):
         size = pair.shape[0]
-        go(copy(part.at[rows(mate % 2, size), :], room.at[0], k_send.at[0], k_recv.at[h, 0], mate, c))
-        landed(room.at[0], k_recv.at[h, 0])
+        go(copy(part.at[rows(mate % 2, size), :], room.at[0], k_send.at[0], k_recv.at[3 * h], mate, c))
+        landed(room.at[0], k_recv.at[3 * h])
         pair[...] = part[rows(r % 2, size), :] + room[0]
 
     def spread(h, step, room, pair, slots):
         for i in slots:
             row, col = lax.rem(r + i // 2 * 2, nrows), across if i % 2 else c
-            go(copy(pair, room.at[i], k_send.at[0], k_recv.at[h, step], row, col))
+            go(copy(pair, room.at[i], k_send.at[0], k_recv.at[3 * h + step], row, col))
 
     def collect(h, step, room, pair, slots):
-        landed(room.at[pl.ds(0, len(slots))], k_recv.at[h, step])
+        landed(room.at[pl.ds(0, len(slots))], k_recv.at[3 * h + step])
         summed = pair[...]
         for i in slots:
             summed = summed + room[i]
@@ -388,11 +388,11 @@
             pltpu.VMEM((tiles, wide, tile), BF16),
             pltpu.VMEM((tiles, width, tile), BF16),
             pltpu.VMEM((tiles, width, tile), BF16),
-            dma((nh + 2,)),
+            dma((3,)),
             dma((1,)), dma((nh, lines)), dma((nh, lines // 2)),
             dma((1,)), dma((nh,)), dma((nh, nrows * group)), dma((nh,)),
             dma((1,)), dma((nh, nrows // 2)),
-            dma((1,)), dma((nh,)), dma((1,)), dma((nh, 3)), dma((1,)),
+            dma((1,)), dma((nh,)), dma((1,)), dma((3 * nh - 1,)), dma((1,)),
         ],
         compiler_params=pltpu.CompilerParams(
             collective_id=0, has_side_effects=True, vmem_limit_bytes=limit),

time: 34.3 us -> 34.3 us (level)
  no operation moved by 1% of the time
where the time goes in v10:
time: 34.3 us; the launch traced here: 33.9 us
  Pallas kernels  33.3 us (97%)
  between operations  0.64 us (2%)
    pallas_call x1, Pallas kernels, per_device(): pl.pallas_call(functools.partial(kernel, nrows, ncols, tile), out_shape=(...  32.1 us
    pallas_call x1, Pallas kernels, per_device(): pl.pallas_call(functools.partial(hand_out, tile), out_shape=(jax.ShapeDty...  1.19 us

profile of v10, /device:TPU:1, one launch (start us, length us, event | category | flops | bytes accessed | tf_op | source)
XLA Modules:
  0.0 33.9 jit_solution(15902438893209780452)
XLA Ops:
  0.6 32.1 %shard_map.50 = (f32[512,256]{1,0:T(8,128)S(1)}, f32[64,256]{1,0:T(8,128)S(1)}, bf16[512,256]{1,0:T(8,128)(2,1)S(1)}, bf16[512,256]{1,0:T(8,128)(2,1)S(1)}, bf16...) custom-call(f32[512,256]{1,0:T(8,128)} %a_hbm.1, f32[64,256]{1,0:T(8,128)} %panel_hbm.1, f32[256,256]{1,0:T(8,128)} %t_hbm.1), custom_call_target="tpu_custom_call" | custom-call | tf_op jit(solution)/shard_map/pallas_call | solution.py:362
  32.7 1.2 %shard_map.51 = (f32[512,256]{1,0:T(8,128)}, f32[64,256]{1,0:T(8,128)}) custom-call(f32[512,256]{1,0:T(8,128)S(1)} %get-tuple-element.8.held_ref, f32[64,256]{1,0:T(8,128)S(1)} %get-tuple-element.9.held_corr_ref, bf16[512,256]{1,0:T(8,128)(2,1)S(1)} %get-tuple-element.10.v_hi, bf16[512,256]{1,0:T(8,128)(2,1)S(1)} %get-tuple-element.11.v_lo, ...), custom_call_target="tpu_custom_call" | custom-call | tf_op jit(solution)/shard_map/pallas_call | solution.py:400
